TPU v7x, 32 devices: a whole 2x2x4 slice. The times are simulated.
32 devices in a mesh: tok: 8 (over z, x), head: 4 (over y, core).
Axes of the slice: x: 2, y: 2, z: 4, core: 2. Of those that a mesh axis runs over, the one named last changes fastest.
Arguments:
- tri_tokens: bfloat16 [4096, 1024], P(('tok', 'head')), may hold values from -6 to 6
- image_tokens: bfloat16 [32768, 1024], P('tok'), may hold values from -6 to 6
- cross_q: bfloat16 [1024, 1024], P(None, 'head'), may hold values from -0.1875 to 0.1875
- cross_kv: bfloat16 [2, 1024, 1024], P(None, None, 'head'), may hold values from -0.1875 to 0.1875
- cross_out: bfloat16 [1024, 1024], P('head'), may hold values from -0.1875 to 0.1875
- self_qkv: bfloat16 [3, 1024, 1024], P(None, None, 'head'), may hold values from -0.1875 to 0.1875
- self_out: bfloat16 [1024, 1024], P('head'), may hold values from -0.1875 to 0.1875
- mlp_in: bfloat16 [1024, 4096], P(None, 'head'), may hold values from -0.1875 to 0.1875
- mlp_out: bfloat16 [4096, 1024], P('head'), may hold values from -0.09375 to 0.09375
Outputs:
- tri_out: bfloat16 [4096, 1024], P(('tok', 'head'))
All inputs are finite; a program needn't handle non-finite values.
Results may differ from a plain program's by a relative error of at most 0.013.
Values may be sent and summed in bfloat16 or wider, within the bound.
A program may use at most 128 MiB of HBM per device.

v0:
```python
import functools
import math

import jax
import jax.numpy as jnp
from jax import lax
from jax.experimental import pallas as pl
from jax.experimental.pallas import tpu as pltpu
from jax.sharding import PartitionSpec as P

HEADS = 16
score_gain = 2.5
VMEM_LIMIT = 56 << 20


def layer_norm(values):
    centered = values - jnp.mean(values, axis=-1, keepdims=True)
    return centered * lax.rsqrt(jnp.mean(centered * centered, axis=-1, keepdims=True) + 1e-05)


def head_scale(product, head_size):
    width = product.shape[1]
    rows = lax.broadcasted_iota(jnp.int32, (width, width), 0) // head_size
    cols = lax.broadcasted_iota(jnp.int32, (width, width), 1) // head_size
    same = (rows == cols).astype(jnp.float32).astype(jnp.bfloat16)
    squares = product * product
    high = squares.astype(jnp.bfloat16)
    low = (squares - high.astype(jnp.float32)).astype(jnp.bfloat16)
    total = jnp.dot(high, same, preferred_element_type=jnp.float32)
    total = total + jnp.dot(low, same, preferred_element_type=jnp.float32)
    return lax.rsqrt(total * (1.0 / head_size) + 1e-06)


def project_kernel(x_ref, w_ref, *out_refs, plan, head_size):
    width = w_ref.shape[2]
    for j, (place, column, factor) in enumerate(plan):
        product = jnp.dot(x_ref[...], w_ref[j], preferred_element_type=jnp.float32)
        if factor is not None:
            product = product * (head_scale(product, head_size) * factor)
        out_refs[place][:, column * width : (column + 1) * width] = product.astype(jnp.bfloat16)


def project(x, weights, plan, head_size):
    rows, depth = x.shape
    count, _, width = weights.shape
    block = math.gcd(rows, 512)
    places = max(p for p, _, _ in plan) + 1
    widths = [width * sum(p == place for p, _, _ in plan) for place in range(places)]
    return pl.pallas_call(
        functools.partial(project_kernel, plan=plan, head_size=head_size),
        out_shape=[jax.ShapeDtypeStruct((rows, w), jnp.bfloat16) for w in widths],
        grid=(rows // block,),
        in_specs=[
            pl.BlockSpec((block, depth), lambda i: (i, 0)),
            pl.BlockSpec((count, depth, width), lambda i: (0, 0, 0)),
        ],
        out_specs=[pl.BlockSpec((block, w), lambda i: (i, 0)) for w in widths],
        compiler_params=pltpu.CompilerParams(vmem_limit_bytes=VMEM_LIMIT),
        cost_estimate=pl.CostEstimate(
            flops=2 * rows * depth * width * count,
            bytes_accessed=2 * (rows * depth + count * depth * width + rows * width * count),
            transcendentals=rows * width,
        ),
    )(x, weights)


def stack_heads(queries, head_size):
    rows, lanes = queries.shape
    lane = lax.broadcasted_iota(jnp.int32, (rows, lanes), 1) // head_size
    zero = jnp.zeros_like(queries)
    heads = lanes // head_size
    if heads == 1:
        return queries
    return jnp.concatenate([jnp.where(lane == h, queries, zero) for h in range(heads)], axis=0)


def pick_heads(acc_ref, rows, lanes, head_size):
    picked = acc_ref[:rows, :]
    lane = lax.broadcasted_iota(jnp.int32, picked.shape, 1) % lanes // head_size
    for h in range(1, lanes // head_size):
        picked = jnp.where(lane == h, acc_ref[h * rows : (h + 1) * rows, :], picked)
    return picked[:, :lanes], picked[:, lanes:]


def fold_keys(stacked, key_of, value_of, acc_ref, key_count, lanes):
    block = math.gcd(key_count, 512)
    ones = jnp.ones((block, lanes), jnp.bfloat16)
    acc_ref[...] = jnp.zeros_like(acc_ref)

    def step(i, carry):
        rows = pl.ds(pl.multiple_of(i * block, block), block)
        scores = lax.dot_general(
            stacked, key_of(rows), (((1,), (1,)), ((), ())), preferred_element_type=jnp.float32
        )
        weights = jnp.exp2(scores).astype(jnp.bfloat16)
        values = jnp.concatenate([value_of(rows), ones], axis=1)
        acc_ref[...] += jnp.dot(weights, values, preferred_element_type=jnp.float32)
        return carry

    lax.fori_loop(0, key_count // block, step, 0, unroll=True)


def attend_kernel(q_ref, k_ref, v_ref, *refs, head_size, finish):
    acc_ref = refs[-1]
    rows, lanes = q_ref.shape
    fold_keys(
        stack_heads(q_ref[...], head_size),
        lambda r: k_ref[r, :],
        lambda r: v_ref[r, :],
        acc_ref,
        k_ref.shape[0],
        lanes,
    )
    mixed, totals = pick_heads(acc_ref, rows, lanes, head_size)
    if finish:
        refs[0][...] = (mixed / totals).astype(jnp.bfloat16)
    else:
        refs[0][...] = mixed.astype(jnp.bfloat16)
        refs[1][...] = totals


def attend(queries, kv, head_size, finish):
    count, width = queries.shape
    keys = kv.shape[0]
    lanes = min(128, width)
    pairs = width // lanes
    block = math.gcd(count, 512)
    outs = [jax.ShapeDtypeStruct((count, width), jnp.bfloat16)]
    if not finish:
        outs.append(jax.ShapeDtypeStruct((count, width), jnp.float32))
    if width % 128:
        keys_values = (kv[:, :width], kv[:, width:])
        shift = 0
    else:
        keys_values = (kv, kv)
        shift = pairs
    result = pl.pallas_call(
        functools.partial(attend_kernel, head_size=head_size, finish=finish),
        out_shape=outs,
        grid=(pairs, count // block),
        in_specs=[
            pl.BlockSpec((block, lanes), lambda p, i: (i, p)),
            pl.BlockSpec((keys, lanes), lambda p, i: (0, p)),
            pl.BlockSpec((keys, lanes), lambda p, i: (0, p + shift)),
        ],
        out_specs=[pl.BlockSpec((block, lanes), lambda p, i: (i, p))] * len(outs),
        scratch_shapes=[pltpu.VMEM((lanes // head_size * block, 2 * lanes), jnp.float32)],
        compiler_params=pltpu.CompilerParams(vmem_limit_bytes=VMEM_LIMIT),
        cost_estimate=pl.CostEstimate(
            flops=16 * count * keys * width,
            bytes_accessed=2 * (3 * count * width + 2 * keys * width),
            transcendentals=count * keys * width // head_size,
        ),
    )(queries, *keys_values)
    return result


def per_device(
    tri_tokens, image_tokens, cross_q, cross_kv, cross_out, self_qkv, self_out, mlp_in, mlp_out,
    *, tok
):
    width = cross_q.shape[1]
    head_size = tri_tokens.shape[1] // HEADS
    head_count = width // head_size
    query_factor = score_gain / math.sqrt(head_size) * math.log2(math.e)

    def spread(stream):
        return lax.all_gather(layer_norm(stream).astype(jnp.bfloat16), "head", axis=0, tiled=True)

    def collect(operand, weight):
        return lax.psum_scatter(
            jnp.dot(operand, weight, preferred_element_type=jnp.float32).astype(jnp.bfloat16),
            "head",
            scatter_dimension=0,
            tiled=True,
        ).astype(jnp.float32)

    stream_zero = tri_tokens.astype(jnp.float32)
    (queries,) = project(spread(stream_zero), cross_q[None], ((0, 0, query_factor),), head_size)
    (view_kv,) = project(image_tokens, cross_kv, ((0, 0, 1.0), (0, 1, None)), head_size)
    all_queries = lax.all_gather(queries, "tok", axis=0, tiled=True)
    weighted, totals = attend(all_queries, view_kv, head_size, False)
    group = queries.shape[0]
    totals = totals.reshape(tok, group, head_count, head_size)[:, :, :, 0]
    totals = totals.transpose(0, 2, 1).astype(jnp.bfloat16)
    weighted = lax.psum_scatter(weighted, "tok", scatter_dimension=0, tiled=True)
    totals = lax.psum_scatter(totals, "tok", scatter_dimension=0, tiled=True)
    totals = jnp.repeat(totals[0].T.astype(jnp.float32), head_size, axis=1)
    mix = (weighted.astype(jnp.float32) / totals).astype(jnp.bfloat16)
    stream_one = stream_zero + collect(mix, cross_out)
    self_queries, self_kv = project(
        spread(stream_one), self_qkv, ((0, 0, query_factor), (1, 0, 1.0), (1, 1, None)), head_size
    )
    all_kv = lax.all_gather(self_kv, "tok", axis=0, tiled=True)
    (mix,) = attend(self_queries, all_kv, head_size, True)
    stream_two = stream_one + collect(mix, self_out)
    hidden = jax.nn.gelu(
        jnp.dot(spread(stream_two), mlp_in, preferred_element_type=jnp.float32), approximate=True
    ).astype(jnp.bfloat16)
    return (stream_two + collect(hidden, mlp_out)).astype(jnp.bfloat16)


def solution(mesh):
    return jax.shard_map(
        functools.partial(per_device, tok=mesh.shape["tok"]),
        mesh=mesh,
        in_specs=(
            P(("tok", "head"), None),
            P("tok", None),
            P(None, "head"),
            P(None, None, "head"),
            P("head", None),
            P(None, None, "head"),
            P("head", None),
            P(None, "head"),
            P("head", None),
        ),
        out_specs=P(("tok", "head"), None),
        check_vma=False,
    )
```

profile of v0, /device:TPU:0, one launch (start us, length us, event | category | flops | bytes accessed | tf_op | source)
XLA Modules:
  0.0 449.6 jit_solution(10217410013275304185)
XLA Ops:
  6.5 0.0 copy-start
  6.5 0.0 all-gather.6.cloned.1.call-start
  6.5 1.2 convert_reduce_fusion
  7.8 1.2 fusion.15
  8.9 1.9 fusion.16
  10.8 0.0 all-gather.6.cloned.1.call-update
  10.8 0.0 all-gather.8.cloned.1.call-start
  10.9 19.5 %all-gather.6.cloned.1.call-done.x_ref = bf16[512,1024]{1,0:T(8,128)(2,1)} async-done(((bf16[128,1024]{1,0:T(8,128)(2,1)}), bf16[512,1024]{1,0:T(8,128)(2,1)}) %all-gather.6.cloned.1.call-update) | async-done | bytes 1048592 | tf_op jit(solution)/shard_map/all_gather | solution.py:168
  30.4 2.9 shard_map.91
  33.3 0.0 all-gather.8.cloned.1.call-update
  33.3 0.0 reduce-scatter.5.cloned.1.call-start
  33.4 13.5 %shard_map.92.k_ref.v_ref = bf16[4096,512]{1,0:T(8,128)(2,1)} custom-call(bf16[4096,1024]{1,0:T(8,128)(2,1)} %x_ref.1, bf16[2,1024,256]{2,1,0:T(8,128)(2,1)} %w_ref.2), custom_call_target="tpu_custom_call" | custom-call | flops 4294967296 | bytes 13631488 | tf_op jit(solution)/shard_map/pallas_call | solution.py:49
  46.9 36.0 %all-gather.8.cloned.1.call-done.q_ref = bf16[4096,256]{1,0:T(8,128)(2,1)} async-done(((bf16[512,256]{1,0:T(8,128)(2,1)}), bf16[4096,256]{1,0:T(8,128)(2,1)}) %all-gather.8.cloned.1.call-update) | async-done | bytes 2097168 | tf_op jit(solution)/shard_map/all_gather | solution.py:181
  82.9 77.3 %shard_map.93 = (bf16[4096,256]{1,0:T(8,128)(2,1)}, f32[4096,256]{1,0:T(8,128)}) custom-call(bf16[4096,256]{1,0:T(8,128)(2,1)} %all-gather.8.cloned.1.call-done.q_ref, bf16[4096,512]{1,0:T(8,128)(2,1)} %shard_map.92.k_ref.v_ref, bf16[4096,512]{1,0:T(8,128)(2,1)} %shard_map.92.k_ref.v_ref), custom_call_target="tpu_custom_call" | custom-call | flops 68719476736 | bytes 10485760 | tf_op jit(solution)/shard_map/pallas_call | solution.py:137
  160.2 0.0 copy-start.5
  160.2 0.0 reduce-scatter.5.cloned.1.call-update
  160.3 0.0 reduce-scatter.7.cloned.1.call-start
  160.3 0.6 copy-done.5
  160.9 0.6 dynamic-slice
  161.5 3.7 convert.6
  165.2 4.3 copy.12
  169.5 2.5 copy.15
  172.0 34.8 %all-reduce = bf16[8,4,512]{2,1,0:T(4,128)(2,1)S(1)} all-reduce(bf16[8,4,512]{2,1,0:T(4,128)(2,1)S(1)} %copy.13), channel_id=3, replica_groups=mesh['tok'=8,'head'=4] {'tok'}, use_global_device_ids=true, to_apply=%region_3.0.clone | all-reduce | flops 16384 | bytes 65536
  206.8 0.7 convert_bitcast_fusion
  207.5 0.1 broadcast_in_dim.5
  207.6 0.2 copy.14
  207.8 0.0 copy-start.1
  207.8 19.0 %reduce-scatter.5.cloned.1.call-done = bf16[512,256]{1,0:T(8,128)(2,1)} async-done(((bf16[4096,256]{1,0:T(8,128)(2,1)}), bf16[512,256]{1,0:T(8,128)(2,1)}) %reduce-scatter.5.cloned.1.call-update) | async-done | bytes 262160 | tf_op jit(solution)/shard_map/reduce_scatter | solution.py:186
  226.8 2.5 convolution_convert_fusion.2
  229.3 0.0 reduce-scatter.7.cloned.1.call-update
  229.3 0.0 all-gather.10.cloned.1.call-start
  229.4 24.0 %reduce-scatter.7.cloned.1.call-done = bf16[128,1024]{1,0:T(8,128)(2,1)} async-done(((bf16[512,1024]{1,0:T(8,128)(2,1)}), bf16[128,1024]{1,0:T(8,128)(2,1)}) %reduce-scatter.7.cloned.1.call-update) | async-done | bytes 262160 | tf_op jit(solution)/shard_map/reduce_scatter | solution.py:171
  253.4 0.0 copy-done.1
  253.4 1.1 fusion.17
  254.5 1.2 multiply_reduce_fusion.1
  255.7 1.8 multiply_convert_fusion.1
  257.4 0.0 all-gather.10.cloned.1.call-update
  257.5 0.0 all-gather.12.cloned.1.call-start
  257.5 16.8 %all-gather.10.cloned.1.call-done.x_ref = bf16[512,1024]{1,0:T(8,128)(2,1)} async-done(((bf16[128,1024]{1,0:T(8,128)(2,1)}), bf16[512,1024]{1,0:T(8,128)(2,1)}) %all-gather.10.cloned.1.call-update) | async-done | bytes 1048592 | tf_op jit(solution)/shard_map/all_gather | solution.py:168
  274.3 4.6 %shard_map.94 = (bf16[512,256]{1,0:T(8,128)(2,1)}, bf16[512,512]{1,0:T(8,128)(2,1)}) custom-call(bf16[512,1024]{1,0:T(8,128)(2,1)} %all-gather.10.cloned.1.call-done.x_ref, bf16[3,1024,256]{2,1,0:T(8,128)(2,1)} %w_ref.3), custom_call_target="tpu_custom_call" | custom-call | flops 805306368 | bytes 3407872 | tf_op jit(solution)/shard_map/pallas_call | solution.py:49
  278.9 0.0 all-gather.12.cloned.1.call-update
  278.9 0.2 reduce-scatter.9.cloned.1.call-start
  279.2 73.3 %all-gather.12.cloned.1.call-done.k_ref.v_ref = bf16[4096,512]{1,0:T(8,128)(2,1)} async-done(((bf16[512,512]{1,0:T(8,128)(2,1)}), bf16[4096,512]{1,0:T(8,128)(2,1)}) %all-gather.12.cloned.1.call-update) | async-done | bytes 4194320 | tf_op jit(solution)/shard_map/all_gather | solution.py:194
  352.5 0.0 copy-start.4
  352.5 11.7 %shard_map.95 = bf16[512,256]{1,0:T(8,128)(2,1)} custom-call(bf16[512,256]{1,0:T(8,128)(2,1)} %get-tuple-element.11.q_ref, bf16[4096,512]{1,0:T(8,128)(2,1)} %all-gather.12.cloned.1.call-done.k_ref.v_ref, bf16[4096,512]{1,0:T(8,128)(2,1)} %all-gather.12.cloned.1.call-done.k_ref.v_ref), custom_call_target="tpu_custom_call" | custom-call | flops 8589934592 | bytes 4980736 | tf_op jit(solution)/shard_map/pallas_call | solution.py:137
  364.1 0.0 copy-done.4
  364.2 2.4 convolution_convert_fusion.1
  366.6 0.0 reduce-scatter.9.cloned.1.call-update
  366.6 0.0 all-gather.14.cloned.1.call-start
  366.6 23.3 %reduce-scatter.9.cloned.1.call-done = bf16[128,1024]{1,0:T(8,128)(2,1)} async-done(((bf16[512,1024]{1,0:T(8,128)(2,1)}), bf16[128,1024]{1,0:T(8,128)(2,1)}) %reduce-scatter.9.cloned.1.call-update) | async-done | bytes 262160 | tf_op jit(solution)/shard_map/reduce_scatter | solution.py:171
  389.9 0.0 copy-done.2
  389.9 1.1 fusion.22
  391.1 1.2 multiply_reduce_fusion
  392.2 1.8 multiply_convert_fusion
  394.0 0.0 all-gather.14.cloned.1.call-update
  394.1 0.0 copy-start.3
  394.1 0.0 reduce-scatter.11.cloned.1.call-start
  394.1 16.8 %all-gather.14.cloned.1.call-done = bf16[512,1024]{1,0:T(8,128)(2,1)} async-done(((bf16[128,1024]{1,0:T(8,128)(2,1)}), bf16[512,1024]{1,0:T(8,128)(2,1)}) %all-gather.14.cloned.1.call-update) | async-done | bytes 1048592 | tf_op jit(solution)/shard_map/all_gather | solution.py:168
  410.9 0.0 copy-done
  410.9 5.3 %convolution_convert_fusion = bf16[512,1024]{1,0:T(8,128)(2,1)} fusion(bf16[1024,1024]{1,0:T(8,128)(2,1)S(1)} %copy-done, bf16[512,1024]{1,0:T(8,128)(2,1)} %all-gather.14.cloned.1.call-done, bf16[1024,1024]{1,0:T(8,128)(2,1)} %param.16), kind=kOutput, calls=%fused_computation.9 | convolution fusion | flops 2152726528 | bytes 6291456 | tf_op jit(solution)/shard_map/dot_general | solution.py:172
  416.2 0.0 reduce-scatter.11.cloned.1.call-update
  416.2 25.0 %reduce-scatter.11.cloned.1.call-done = bf16[128,1024]{1,0:T(8,128)(2,1)} async-done(((bf16[512,1024]{1,0:T(8,128)(2,1)}), bf16[128,1024]{1,0:T(8,128)(2,1)}) %reduce-scatter.11.cloned.1.call-update) | async-done | bytes 262160 | tf_op jit(solution)/shard_map/reduce_scatter | solution.py:171
  441.3 0.0 copy-done.3
  441.3 1.8 add_convert_fusion
  (9 shorter events, 0.1 us)
Async XLA Ops:
  6.5 404.4 %copy-start = (bf16[1024,1024]{1,0:T(8,128)(2,1)S(1)}, bf16[1024,1024]{1,0:T(8,128)(2,1)}, u32[]{:S(2)}) copy-start(bf16[1024,1024]{1,0:T(8,128)(2,1)} %param.17) | copy-start | bytes 6291460
  6.5 23.9 %all-gather.6.cloned.1.call-start = ((), (), s32[]{:S(2)}) async-start(), calls=%async_computation.4 | async-start | bytes 1310720 | tf_op jit(solution)/shard_map/all_gather | solution.py:168
  10.8 72.1 %all-gather.8.cloned.1.call-start = ((), (), s32[]{:S(2)}) async-start(), calls=%async_computation.5 | async-start | bytes 2359296 | tf_op jit(solution)/shard_map/all_gather | solution.py:181
  33.3 193.5 %reduce-scatter.5.cloned.1.call-start = ((), (), s32[]{:S(2)}) async-start(), calls=%async_computation.6 | async-start | bytes 2359296 | tf_op jit(solution)/shard_map/reduce_scatter | solution.py:186
  160.2 0.7 copy-start.5
  160.3 93.1 %reduce-scatter.7.cloned.1.call-start = ((), (), s32[]{:S(2)}) async-start(), calls=%async_computation.7 | async-start | bytes 1310720 | tf_op jit(solution)/shard_map/reduce_scatter | solution.py:171
  207.8 45.6 %copy-start.1 = (bf16[128,1024]{1,0:T(8,128)(2,1)S(1)}, bf16[128,1024]{1,0:T(8,128)(2,1)}, u32[]{:S(2)}) copy-start(bf16[128,1024]{1,0:T(8,128)(2,1)} %param.9) | copy-start | bytes 786436
  229.3 45.0 %all-gather.10.cloned.1.call-start = ((), (), s32[]{:S(2)}) async-start(), calls=%async_computation.8 | async-start | bytes 1310720 | tf_op jit(solution)/shard_map/all_gather | solution.py:168
  257.5 95.0 %all-gather.12.cloned.1.call-start = ((), (), s32[]{:S(2)}) async-start(), calls=%async_computation.9 | async-start | bytes 4718592 | tf_op jit(solution)/shard_map/all_gather | solution.py:194
  278.9 111.0 %reduce-scatter.9.cloned.1.call-start = ((), (), s32[]{:S(2)}) async-start(), calls=%async_computation.10 | async-start | bytes 1310720 | tf_op jit(solution)/shard_map/reduce_scatter | solution.py:171
  352.5 11.7 %copy-start.4 = (bf16[256,1024]{1,0:T(8,128)(2,1)S(1)}, bf16[256,1024]{1,0:T(8,128)(2,1)}, u32[]{:S(2)}) copy-start(bf16[256,1024]{1,0:T(8,128)(2,1)} %param.15) | copy-start | bytes 1572868
  364.2 25.8 %copy-start.2 = (bf16[128,1024]{1,0:T(8,128)(2,1)S(1)}, bf16[128,1024]{1,0:T(8,128)(2,1)}, u32[]{:S(2)}) copy-start(bf16[128,1024]{1,0:T(8,128)(2,1)} %reduce-scatter.7.cloned.1.call-done) | copy-start | bytes 786436
  366.6 44.4 %all-gather.14.cloned.1.call-start = ((), (), s32[]{:S(2)}) async-start(), calls=%async_computation.11 | async-start | bytes 1310720 | tf_op jit(solution)/shard_map/all_gather | solution.py:168
  394.1 47.2 %copy-start.3 = (bf16[128,1024]{1,0:T(8,128)(2,1)S(1)}, bf16[128,1024]{1,0:T(8,128)(2,1)}, u32[]{:S(2)}) copy-start(bf16[128,1024]{1,0:T(8,128)(2,1)} %reduce-scatter.9.cloned.1.call-done) | copy-start | bytes 786436
  394.1 47.2 %reduce-scatter.11.cloned.1.call-start = ((), (), s32[]{:S(2)}) async-start(), calls=%async_computation.12 | async-start | bytes 1310720 | tf_op jit(solution)/shard_map/reduce_scatter | solution.py:171
Sparse Core Ops, SparseCore 0:
  11.0 19.4 all-gather.5
  33.4 49.4 all-gather.7
  160.4 66.3 reduce-scatter.4
  229.5 23.8 reduce-scatter.6
  257.6 16.6 all-gather.9
  279.0 73.3 all-gather.11
  366.7 23.1 reduce-scatter.8
  394.2 16.7 all-gather.13
  416.4 24.8 reduce-scatter.10
where the time goes:
time: 451 us; the launch traced here: 450 us
  waiting for transfers between devices  254 us (56%)
  Pallas kernels  110 us (24%)
  blocking collectives  34.8 us (8%)
  other arithmetic  18.6 us (4%)
  between operations  13.3 us (3%)
  matrix products  10.2 us (2%)
  local copies, waits for them, and re-layouts  8.25 us (2%)
    pallas_call x2, Pallas kernels, attend(): pl.pallas_call(functools.partial(attend_kernel, head_size=head_size, fini...  89 us
    all_gather x1, waiting for transfers between devices, per_device(): all_kv = lax.all_gather(self_kv, 'tok', axis=0, tiled=True)  73.3 us
    reduce_scatter x3, waiting for transfers between devices, collect(): lax.psum_scatter(jnp.dot(operand, weight, preferred_element_type=jnp.floa...  72.3 us
    all_gather x3, waiting for transfers between devices, spread(): lax.all_gather(layer_norm(stream).astype(jnp.bfloat16), 'head', axis=0, t...  53.2 us
    all_gather x1, waiting for transfers between devices, per_device(): all_queries = lax.all_gather(queries, 'tok', axis=0, tiled=True)  36 us
    unnamed x1, blocking collectives  34.8 us
    pallas_call x3, Pallas kernels, project(): pl.pallas_call(functools.partial(project_kernel, plan=plan, head_size=hea...  21 us
    reduce_scatter x1, waiting for transfers between devices, per_device(): lax.psum_scatter(weighted, 'tok', scatter_dimension=0, tiled=True)  19 us
  transfers between devices with their start and end apart: 9, of which 9 were waited for; matrix products, arithmetic and copies ran while one was open for 3% of the time, Pallas kernels for 3%

commit v1 on v0

--- a/solution.py
+++ b/solution.py
@@ -10,25 +10,337 @@
 
 HEADS = 16
 score_gain = 2.5
-VMEM_LIMIT = 56 << 20
+VMEM_LIMIT = 60 << 20
+MESH = pl.DeviceIdType.MESH
+ONES = 16
+bf16 = jnp.bfloat16
+f32 = jnp.float32
 
 
 def layer_norm(values):
     centered = values - jnp.mean(values, axis=-1, keepdims=True)
     return centered * lax.rsqrt(jnp.mean(centered * centered, axis=-1, keepdims=True) + 1e-05)
+
+
+def dot(a, b):
+    return jnp.dot(a, b, preferred_element_type=f32)
 
 
 def head_scale(product, head_size):
     width = product.shape[1]
     rows = lax.broadcasted_iota(jnp.int32, (width, width), 0) // head_size
     cols = lax.broadcasted_iota(jnp.int32, (width, width), 1) // head_size
-    same = (rows == cols).astype(jnp.float32).astype(jnp.bfloat16)
+    same = (rows == cols).astype(f32).astype(bf16)
     squares = product * product
-    high = squares.astype(jnp.bfloat16)
-    low = (squares - high.astype(jnp.float32)).astype(jnp.bfloat16)
-    total = jnp.dot(high, same, preferred_element_type=jnp.float32)
-    total = total + jnp.dot(low, same, preferred_element_type=jnp.float32)
+    high = squares.astype(bf16)
+    low = (squares - high.astype(f32)).astype(bf16)
+    total = dot(high, same) + dot(low, same)
     return lax.rsqrt(total * (1.0 / head_size) + 1e-06)
+
+
+def head_norm_rows(product, head_size, factor):
+    width, count = product.shape
+    shaped = product.reshape(width // head_size, head_size, count)
+    mean = jnp.sum(shaped * shaped, axis=1, keepdims=True) * (1.0 / head_size)
+    return (shaped * (lax.rsqrt(mean + 1e-06) * factor)).reshape(width, count)
+
+
+def send(source, target, send_sem, recv_sem, device):
+    copy = pltpu.make_async_remote_copy(
+        src_ref=source,
+        dst_ref=target,
+        send_sem=send_sem,
+        recv_sem=recv_sem,
+        device_id=device,
+        device_id_type=MESH,
+    )
+    return copy
+
+
+def greet(devices):
+    barrier = pltpu.get_barrier_semaphore()
+    for device in devices:
+        pl.semaphore_signal(barrier, inc=1, device_id=device, device_id_type=MESH)
+    pl.semaphore_wait(barrier, len(devices))
+
+
+class Place:
+    def __init__(self, toks, heads):
+        self.toks, self.heads = toks, heads
+        self.tok, self.head = lax.axis_index("tok"), lax.axis_index("head")
+        self.pairs = heads // 2
+        self.pair, self.core = lax.div(self.head, 2), lax.rem(self.head, 2)
+
+    def partner(self):
+        return (self.tok, self.pair * 2 + 1 - self.core)
+
+    def pair_at(self, k):
+        return lax.rem(self.pair + k + self.pairs, self.pairs)
+
+    def across(self, k):
+        return (self.tok, self.pair_at(k) * 2 + self.core)
+
+    def head_peers(self):
+        return [self.partner()] + [self.across(k) for k in range(1, self.pairs)]
+
+
+class Gather:
+    @staticmethod
+    def scratch(heads, rows, depth):
+        dma = pltpu.SemaphoreType.DMA((heads // 2,))
+        return [pltpu.VMEM((heads, rows, depth), bf16), dma, dma, dma, dma]
+
+    def __init__(self, place, refs):
+        self.place = place
+        self.rows, self.pair_out, self.pair_in, self.far_out, self.far_in = refs
+
+    def far(self, k):
+        p = self.place
+        mine = self.rows.at[p.head]
+        return send(mine, mine, self.far_out.at[k], self.far_in.at[k], p.across(k))
+
+    def far_arrival(self, k):
+        p = self.place
+        slot = self.rows.at[p.pair_at(-k) * 2 + p.core]
+        return send(slot, slot, self.far_out.at[k], self.far_in.at[k], p.across(-k))
+
+    def near(self, k):
+        p = self.place
+        slot = self.rows.at[p.pair_at(-k) * 2 + p.core]
+        return send(slot, slot, self.pair_out.at[k], self.pair_in.at[k], p.partner())
+
+    def near_arrival(self, k):
+        p = self.place
+        slot = self.rows.at[p.pair_at(-k) * 2 + 1 - p.core]
+        return send(slot, slot, self.pair_out.at[k], self.pair_in.at[k], p.partner())
+
+    def start(self, value):
+        self.rows[self.place.head] = value
+        for k in range(1, self.place.pairs):
+            self.far(k).start()
+        self.near(0).start()
+
+    def forward(self):
+        for k in range(1, self.place.pairs):
+            self.far_arrival(k).wait_recv()
+            self.near(k).start()
+
+    def finish(self):
+        for k in range(self.place.pairs):
+            self.near_arrival(k).wait_recv()
+
+    def drain(self):
+        for k in range(1, self.place.pairs):
+            self.far(k).wait_send()
+        for k in range(self.place.pairs):
+            self.near(k).wait_send()
+
+
+def join(tiles, width):
+    total = functools.reduce(lambda a, b: a + b, [t.astype(f32) for t in tiles])
+    return total[:width], total[width : width + 8] + total[width + 8 : width + 16]
+
+
+def pack(mixed, totals):
+    high = totals.astype(bf16).astype(f32)
+    return jnp.concatenate([mixed, high, totals - high], axis=0).astype(bf16)
+
+
+def attend_block(queries, k_ref, vt_ref, head_size):
+    width, count = queries.shape
+    lanes = min(128, width)
+    keys = k_ref.shape[0]
+    block = math.gcd(keys, 2048)
+    row = lax.broadcasted_iota(jnp.int32, (lanes, count), 0) // head_size
+    place = lax.broadcasted_iota(jnp.int32, (ONES, count), 0) % 8
+    mixed, totals = [], jnp.zeros((ONES, count), f32)
+    for h in range(width // head_size):
+        first = h * head_size // lanes * lanes
+        picked = queries[first : first + lanes]
+        if lanes > head_size:
+            picked = jnp.where(row == h % (lanes // head_size), picked, jnp.zeros_like(picked))
+        acc = jnp.zeros((head_size + ONES, count), f32)
+        for i in range(keys // block):
+            rows = slice(i * block, (i + 1) * block)
+            scores = dot(k_ref[rows, first : first + lanes], picked)
+            acc = acc + dot(vt_ref[h, :, rows], jnp.exp2(scores).astype(bf16))
+        mixed.append(acc[:head_size])
+        totals = jnp.where(place == h, acc[head_size:], totals)
+    return pack(jnp.concatenate(mixed, axis=0), totals[:8])
+
+
+def cross_kernel(
+    tri_ref, image_ref, wq_ref, wkv_ref, out_ref,
+    image, k_ref, vt_ref, queries, tiles, pair_tiles, joined, far_tiles,
+    image_sem, q_out, q_in, f_out, f_in, p_out, p_in, c_out, c_in, *gather_refs,
+    toks, heads, head_size, factor,
+):
+    place = Place(toks, heads)
+    width, group = out_ref.shape
+    lines = toks // 2
+    line, side = lax.div(place.tok, 2), lax.rem(place.tok, 2)
+    neighbour = (line * 2 + 1 - side, place.head)
+
+    def line_at(k):
+        return lax.rem(line + k + lines, lines)
+
+    def peer(k):
+        return (line_at(k) * 2 + side, place.head)
+
+    keys = k_ref.shape[0]
+    step_rows = math.gcd(keys, 512)
+    steps = keys // step_rows
+
+    def fetch(i):
+        rows = pl.ds(pl.multiple_of(i * step_rows, step_rows), step_rows)
+        return pltpu.make_async_copy(image_ref.at[rows], image.at[rows], image_sem.at[i])
+
+    for i in range(steps):
+        fetch(i).start()
+    greet(place.head_peers() + [neighbour] + [peer(k) for k in range(1, lines)])
+    gather = Gather(place, gather_refs)
+    gather.start(layer_norm(tri_ref[...].astype(f32)).astype(bf16))
+    vt_ref[:, head_size:, :] = jnp.ones((width // head_size, ONES, keys), bf16)
+
+    def q_send(k):
+        mine = queries.at[place.tok]
+        return send(mine, mine, q_out.at[k], q_in.at[k], peer(-k) if k else neighbour)
+
+    def q_arrival(k):
+        slot = queries.at[line_at(k) * 2 + side]
+        return send(slot, slot, q_out.at[k], q_in.at[k], peer(k))
+
+    def project(i, carry):
+        @pl.when(i == steps // 2)
+        def _():
+            gather.forward()
+
+        @pl.when(i == steps * 3 // 4)
+        def _():
+            gather.finish()
+            x = gather.rows[...].reshape(group, -1)
+            product = jnp.transpose(dot(x, wq_ref[...]))
+            queries[place.tok] = head_norm_rows(product, head_size, factor).astype(bf16)
+            if lines > 1:
+                q_send(1).start()
+
+        rows = pl.ds(pl.multiple_of(i * step_rows, step_rows), step_rows)
+        fetch(i).wait()
+        x = image[rows, :]
+        k = dot(x, wkv_ref[0])
+        k_ref[rows, :] = (k * head_scale(k, head_size)).astype(bf16)
+        v = jnp.transpose(dot(x, wkv_ref[1])).astype(bf16)
+        vt_ref[:, :head_size, rows] = v.reshape(width // head_size, head_size, step_rows)
+        return carry
+
+    lax.fori_loop(0, steps, project, 0)
+    for k in range(2, lines):
+        q_send(k).start()
+    q_send(0).start()
+
+    def forward(k, slot):
+        block = queries.at[slot]
+        return send(block, block, f_out.at[k], f_in.at[k], neighbour)
+
+    def pair_send(k, s):
+        return send(tiles.at[s], pair_tiles.at[k], p_out.at[k], p_in.at[k], neighbour)
+
+    def far_send(k):
+        return send(joined.at[k], far_tiles.at[k], c_out.at[k], c_in.at[k], peer(k))
+
+    def attend(s, carry):
+        k = lax.div(s, 2) + 1
+        last = k == lines
+        first = lax.rem(s, 2) == 0
+        mine = first != last
+        slot = lax.rem(line + k, lines) * 2 + jnp.where(mine, side, 1 - side)
+
+        @pl.when(jnp.logical_and(first, jnp.logical_not(last)))
+        def _():
+            block = queries.at[slot]
+            send(block, block, q_out.at[k], q_in.at[k], neighbour).wait_recv()
+            forward(k, slot).start()
+
+        @pl.when(jnp.logical_and(jnp.logical_not(first), jnp.logical_not(last)))
+        def _():
+            forward(k, slot).wait_recv()
+
+        @pl.when(jnp.logical_and(first, last))
+        def _():
+            block = queries.at[slot]
+            send(block, block, q_out.at[0], q_in.at[0], neighbour).wait_recv()
+
+        tiles[s] = attend_block(queries[slot], k_ref, vt_ref, head_size)
+
+        @pl.when(jnp.logical_not(mine))
+        def _():
+            pair_send(k, s).start()
+
+        @pl.when(jnp.logical_and(first, k > 1))
+        def _():
+            before = k - 1
+            pair_send(before, s).wait_recv()
+            joined[before] = pack(*join([tiles[2 * before - 2], pair_tiles[before]], width))
+            far_send(before).start()
+
+        return carry
+
+    lax.fori_loop(0, 2 * lines, attend, 0)
+    pair_send(lines, 0).wait_recv()
+    for k in range(1, lines):
+        far_send(k).wait_recv()
+    mixed, totals = join(
+        [tiles[2 * lines - 1], pair_tiles[lines]] + [far_tiles[k] for k in range(1, lines)], width
+    )
+    for h in range(width // head_size):
+        rows = slice(h * head_size, (h + 1) * head_size)
+        out_ref[rows, :] = (mixed[rows] / totals[h : h + 1]).astype(bf16)
+    gather.drain()
+    for k in range(lines):
+        q_send(k).wait_send()
+    for k in range(1, lines):
+        forward(k, 0).wait_send()
+        far_send(k).wait_send()
+    for k in range(1, lines + 1):
+        pair_send(k, 0).wait_send()
+
+
+def cross(tri, image, wq, wkv, toks, heads, head_size, factor):
+    rows, depth = tri.shape
+    keys = image.shape[0]
+    width = wq.shape[1]
+    group = rows * heads
+    lines = toks // 2
+    tile = (width + 16, group)
+    vmem = pl.BlockSpec(memory_space=pltpu.VMEM)
+    dma = pltpu.SemaphoreType.DMA
+    return pl.pallas_call(
+        functools.partial(
+            cross_kernel, toks=toks, heads=heads, head_size=head_size, factor=factor
+        ),
+        out_shape=jax.ShapeDtypeStruct((width, group), bf16),
+        in_specs=[vmem, pl.BlockSpec(memory_space=pl.ANY), vmem, vmem],
+        out_specs=vmem,
+        scratch_shapes=[
+            pltpu.VMEM((keys, depth), bf16),
+            pltpu.VMEM((keys, width), bf16),
+            pltpu.VMEM((width // head_size, head_size + ONES, keys), bf16),
+            pltpu.VMEM((toks, width, group), bf16),
+            pltpu.VMEM((2 * lines,) + tile, bf16),
+            pltpu.VMEM((lines + 1,) + tile, bf16),
+            pltpu.VMEM((lines,) + tile, bf16),
+            pltpu.VMEM((lines,) + tile, bf16),
+            dma((keys // math.gcd(keys, 512),)),
+            dma((lines,)), dma((lines,)),
+            dma((lines,)), dma((lines,)),
+            dma((lines + 1,)), dma((lines + 1,)),
+            dma((lines,)), dma((lines,)),
+        ] + Gather.scratch(heads, rows, depth),
+        compiler_params=pltpu.CompilerParams(
+            vmem_limit_bytes=VMEM_LIMIT, collective_id=0, has_side_effects=True
+        ),
+        name="cross",
+    )(tri, image, wq, wkv)
 
 
 def project_kernel(x_ref, w_ref, *out_refs, plan, head_size):
@@ -157,11 +469,10 @@
 
 def per_device(
     tri_tokens, image_tokens, cross_q, cross_kv, cross_out, self_qkv, self_out, mlp_in, mlp_out,
-    *, tok
+    *, tok, head
 ):
     width = cross_q.shape[1]
     head_size = tri_tokens.shape[1] // HEADS
-    head_count = width // head_size
     query_factor = score_gain / math.sqrt(head_size) * math.log2(math.e)
 
     def spread(stream):
@@ -176,17 +487,8 @@
         ).astype(jnp.float32)
 
     stream_zero = tri_tokens.astype(jnp.float32)
-    (queries,) = project(spread(stream_zero), cross_q[None], ((0, 0, query_factor),), head_size)
-    (view_kv,) = project(image_tokens, cross_kv, ((0, 0, 1.0), (0, 1, None)), head_size)
-    all_queries = lax.all_gather(queries, "tok", axis=0, tiled=True)
-    weighted, totals = attend(all_queries, view_kv, head_size, False)
-    group = queries.shape[0]
-    totals = totals.reshape(tok, group, head_count, head_size)[:, :, :, 0]
-    totals = totals.transpose(0, 2, 1).astype(jnp.bfloat16)
-    weighted = lax.psum_scatter(weighted, "tok", scatter_dimension=0, tiled=True)
-    totals = lax.psum_scatter(totals, "tok", scatter_dimension=0, tiled=True)
-    totals = jnp.repeat(totals[0].T.astype(jnp.float32), head_size, axis=1)
-    mix = (weighted.astype(jnp.float32) / totals).astype(jnp.bfloat16)
+    mixed = cross(tri_tokens, image_tokens, cross_q, cross_kv, tok, head, head_size, query_factor)
+    mix = mixed.T
     stream_one = stream_zero + collect(mix, cross_out)
     self_queries, self_kv = project(
         spread(stream_one), self_qkv, ((0, 0, query_factor), (1, 0, 1.0), (1, 1, None)), head_size
@@ -202,7 +504,7 @@
 
 def solution(mesh):
     return jax.shard_map(
-        functools.partial(per_device, tok=mesh.shape["tok"]),
+        functools.partial(per_device, tok=mesh.shape["tok"], head=mesh.shape["head"]),
         mesh=mesh,
         in_specs=(
             P(("tok", "head"), None),

time: 451 us -> 335 us (0.74)
  waiting for transfers between devices: 254 us -> 179 us
  blocking collectives: 34.8 us -> 0 us
  Pallas kernels: 110 us -> 122 us
  other arithmetic: 18.6 us -> 9.98 us
  local copies, waits for them, and re-layouts: 8.25 us -> 0.03 us
    pallas_call x0 -> x1, Pallas kernels: none -> 106 us  [cross(): pl.pallas_call(functools.partial(cross_kernel, toks=toks, heads=heads, he...]
    pallas_call x2 -> x1, Pallas kernels: 89 us -> 11.7 us  [attend(): pl.pallas_call(functools.partial(attend_kernel, head_size=head_size, fini...]
    all_gather x1 -> x0, waiting for transfers between devices: 36 us -> none  [per_device(): all_queries = lax.all_gather(queries, 'tok', axis=0, tiled=True)]
    unnamed x1 -> x0, blocking collectives: 34.8 us -> none
    all_gather x3 -> x2, waiting for transfers between devices: 53.2 us -> 33.7 us  [spread(): lax.all_gather(layer_norm(stream).astype(jnp.bfloat16), 'head', axis=0, t...]
    reduce_scatter x1 -> x0, waiting for transfers between devices: 19 us -> none  [per_device(): lax.psum_scatter(weighted, 'tok', scatter_dimension=0, tiled=True)]
    pallas_call x3 -> x1, Pallas kernels: 21 us -> 4.6 us  [project(): pl.pallas_call(functools.partial(project_kernel, plan=plan, head_size=hea...]
  transfers between devices with their start and end apart: 9 -> 6, of which waited for: 9 -> 6; matrix products, arithmetic and copies ran while one was open for 3% -> 0% of each run, Pallas kernels for 3% -> 0%
where the time goes in v1:
time: 335 us
  waiting for transfers between devices  179 us (53%)
  Pallas kernels  122 us (36%)
  between operations  13.5 us (4%)
  matrix products  10.1 us (3%)
  other arithmetic  9.98 us (3%)
    pallas_call x1, Pallas kernels, cross(): pl.pallas_call(functools.partial(cross_kernel, toks=toks, heads=heads, he...  106 us
    all_gather x1, waiting for transfers between devices, per_device(): all_kv = lax.all_gather(self_kv, 'tok', axis=0, tiled=True)  73.3 us
    reduce_scatter x3, waiting for transfers between devices, collect(): lax.psum_scatter(jnp.dot(operand, weight, preferred_element_type=jnp.floa...  71.9 us
    all_gather x2, waiting for transfers between devices, spread(): lax.all_gather(layer_norm(stream).astype(jnp.bfloat16), 'head', axis=0, t...  33.7 us
    pallas_call x1, Pallas kernels, attend(): pl.pallas_call(functools.partial(attend_kernel, head_size=head_size, fini...  11.7 us
    dot_general x3, matrix products, collect(): jnp.dot(operand, weight, preferred_element_type=jnp.float32)  10.1 us
  transfers between devices with their start and end apart: 6, of which 6 were waited for; matrix products, arithmetic and copies ran while one was open for 0% of the time, Pallas kernels for 0%

profile of v1, /device:TPU:0, one launch (start us, length us, event | category | flops | bytes accessed | tf_op | source)
XLA Modules:
  0.0 335.0 jit_solution(7355581054185431724)
XLA Ops:
  6.5 0.0 copy-start
  6.5 0.0 copy-start.4
  6.5 0.0 reduce-scatter.4.cloned.1.call-start
  6.5 105.8 %cross.1 = bf16[256,512]{1,0:T(8,128)(2,1)} custom-call(bf16[128,1024]{1,0:T(8,128)(2,1)} %tri_ref.1, bf16[4096,1024]{1,0:T(8,128)(2,1)} %image_ref.1, bf16[1024,256]{1,0:T(8,128)(2,1)} %wq_ref.1, bf16[2,1024,256]{2,1,0:T(8,128)(2,1)} %wkv_ref.1), custom_call_target="tpu_custom_call" | custom-call | tf_op jit(solution)/shard_map/cross/pallas_call | solution.py:317
  112.3 0.0 copy-done.4
  112.3 0.0 copy-start.1
  112.3 2.4 convolution_convert_fusion.2
  114.8 0.0 reduce-scatter.4.cloned.1.call-update
  114.8 0.0 all-gather.4.cloned.1.call-start
  114.8 23.6 %reduce-scatter.4.cloned.1.call-done = bf16[128,1024]{1,0:T(8,128)(2,1)} async-done(((bf16[512,1024]{1,0:T(8,128)(2,1)}), bf16[128,1024]{1,0:T(8,128)(2,1)}) %reduce-scatter.4.cloned.1.call-update) | async-done | bytes 262160 | tf_op jit(solution)/shard_map/reduce_scatter | solution.py:482
  138.4 0.0 copy-done.1
  138.4 1.1 fusion.13
  139.5 1.2 multiply_reduce_fusion.1
  140.7 1.8 multiply_convert_fusion.1
  142.5 0.0 all-gather.4.cloned.1.call-update
  142.5 0.0 all-gather.6.cloned.1.call-start
  142.5 16.8 %all-gather.4.cloned.1.call-done.x_ref = bf16[512,1024]{1,0:T(8,128)(2,1)} async-done(((bf16[128,1024]{1,0:T(8,128)(2,1)}), bf16[512,1024]{1,0:T(8,128)(2,1)}) %all-gather.4.cloned.1.call-update) | async-done | bytes 1048592 | tf_op jit(solution)/shard_map/all_gather | solution.py:479
  159.4 4.6 %shard_map.91 = (bf16[512,256]{1,0:T(8,128)(2,1)}, bf16[512,512]{1,0:T(8,128)(2,1)}) custom-call(bf16[512,1024]{1,0:T(8,128)(2,1)} %all-gather.4.cloned.1.call-done.x_ref, bf16[3,1024,256]{2,1,0:T(8,128)(2,1)} %w_ref.1), custom_call_target="tpu_custom_call" | custom-call | flops 805306368 | bytes 3407872 | tf_op jit(solution)/shard_map/pallas_call | solution.py:361
  164.0 0.0 all-gather.6.cloned.1.call-update
  164.0 0.2 reduce-scatter.6.cloned.1.call-start
  164.2 73.3 %all-gather.6.cloned.1.call-done.k_ref.v_ref = bf16[4096,512]{1,0:T(8,128)(2,1)} async-done(((bf16[512,512]{1,0:T(8,128)(2,1)}), bf16[4096,512]{1,0:T(8,128)(2,1)}) %all-gather.6.cloned.1.call-update) | async-done | bytes 4194320 | tf_op jit(solution)/shard_map/all_gather | solution.py:496
  237.6 0.0 copy-start.5
  237.6 11.7 %shard_map.92 = bf16[512,256]{1,0:T(8,128)(2,1)} custom-call(bf16[512,256]{1,0:T(8,128)(2,1)} %get-tuple-element.7.q_ref, bf16[4096,512]{1,0:T(8,128)(2,1)} %all-gather.6.cloned.1.call-done.k_ref.v_ref, bf16[4096,512]{1,0:T(8,128)(2,1)} %all-gather.6.cloned.1.call-done.k_ref.v_ref), custom_call_target="tpu_custom_call" | custom-call | flops 8589934592 | bytes 4980736 | tf_op jit(solution)/shard_map/pallas_call | solution.py:449
  249.2 0.0 copy-done.5
  249.2 0.0 copy-start.2
  249.2 2.4 convolution_convert_fusion.1
  251.6 0.0 reduce-scatter.6.cloned.1.call-update
  251.6 0.0 all-gather.8.cloned.1.call-start
  251.7 23.2 %reduce-scatter.6.cloned.1.call-done = bf16[128,1024]{1,0:T(8,128)(2,1)} async-done(((bf16[512,1024]{1,0:T(8,128)(2,1)}), bf16[128,1024]{1,0:T(8,128)(2,1)}) %reduce-scatter.6.cloned.1.call-update) | async-done | bytes 262160 | tf_op jit(solution)/shard_map/reduce_scatter | solution.py:482
  274.9 0.0 copy-done.2
  274.9 1.1 fusion.18
  276.1 1.2 multiply_reduce_fusion
  277.3 1.8 multiply_convert_fusion
  279.1 0.0 all-gather.8.cloned.1.call-update
  279.1 0.0 copy-start.3
  279.1 0.0 reduce-scatter.8.cloned.1.call-start
  279.1 16.8 %all-gather.8.cloned.1.call-done = bf16[512,1024]{1,0:T(8,128)(2,1)} async-done(((bf16[128,1024]{1,0:T(8,128)(2,1)}), bf16[512,1024]{1,0:T(8,128)(2,1)}) %all-gather.8.cloned.1.call-update) | async-done | bytes 1048592 | tf_op jit(solution)/shard_map/all_gather | solution.py:479
  296.0 0.0 copy-done
  296.0 5.3 %convolution_convert_fusion = bf16[512,1024]{1,0:T(8,128)(2,1)} fusion(bf16[1024,1024]{1,0:T(8,128)(2,1)S(1)} %copy-done, bf16[512,1024]{1,0:T(8,128)(2,1)} %all-gather.8.cloned.1.call-done, bf16[1024,1024]{1,0:T(8,128)(2,1)} %param.16), kind=kOutput, calls=%fused_computation.9 | convolution fusion | flops 2152726528 | bytes 6291456 | tf_op jit(solution)/shard_map/dot_general | solution.py:483
  301.2 0.0 reduce-scatter.8.cloned.1.call-update
  301.3 25.0 %reduce-scatter.8.cloned.1.call-done = bf16[128,1024]{1,0:T(8,128)(2,1)} async-done(((bf16[512,1024]{1,0:T(8,128)(2,1)}), bf16[128,1024]{1,0:T(8,128)(2,1)}) %reduce-scatter.8.cloned.1.call-update) | async-done | bytes 262160 | tf_op jit(solution)/shard_map/reduce_scatter | solution.py:482
  326.3 0.0 copy-done.3
  326.3 1.8 add_convert_fusion
  (4 shorter events, 0.0 us)
Async XLA Ops:
  6.5 289.4 %copy-start = (bf16[1024,1024]{1,0:T(8,128)(2,1)S(1)}, bf16[1024,1024]{1,0:T(8,128)(2,1)}, u32[]{:S(2)}) copy-start(bf16[1024,1024]{1,0:T(8,128)(2,1)} %param.17) | copy-start | bytes 6291460
  6.5 105.8 %copy-start.4 = (bf16[256,1024]{1,0:T(8,128)(2,1)S(1)}, bf16[256,1024]{1,0:T(8,128)(2,1)}, u32[]{:S(2)}) copy-start(bf16[256,1024]{1,0:T(8,128)(2,1)} %param.13) | copy-start | bytes 1572868
  6.5 131.9 %reduce-scatter.4.cloned.1.call-start = ((), (), s32[]{:S(2)}) async-start(), calls=%async_computation.3 | async-start | bytes 1310720 | tf_op jit(solution)/shard_map/reduce_scatter | solution.py:482
  112.3 26.1 %copy-start.1 = (bf16[128,1024]{1,0:T(8,128)(2,1)S(1)}, bf16[128,1024]{1,0:T(8,128)(2,1)}, u32[]{:S(2)}) copy-start(bf16[128,1024]{1,0:T(8,128)(2,1)} %tri_ref.1) | copy-start | bytes 786436
  114.8 44.6 %all-gather.4.cloned.1.call-start = ((), (), s32[]{:S(2)}) async-start(), calls=%async_computation.4 | async-start | bytes 1310720 | tf_op jit(solution)/shard_map/all_gather | solution.py:479
  142.5 95.1 %all-gather.6.cloned.1.call-start = ((), (), s32[]{:S(2)}) async-start(), calls=%async_computation.5 | async-start | bytes 4718592 | tf_op jit(solution)/shard_map/all_gather | solution.py:496
  164.0 110.9 %reduce-scatter.6.cloned.1.call-start = ((), (), s32[]{:S(2)}) async-start(), calls=%async_computation.6 | async-start | bytes 1310720 | tf_op jit(solution)/shard_map/reduce_scatter | solution.py:482
  237.6 11.7 %copy-start.5 = (bf16[256,1024]{1,0:T(8,128)(2,1)S(1)}, bf16[256,1024]{1,0:T(8,128)(2,1)}, u32[]{:S(2)}) copy-start(bf16[256,1024]{1,0:T(8,128)(2,1)} %param.15) | copy-start | bytes 1572868
  249.2 25.7 %copy-start.2 = (bf16[128,1024]{1,0:T(8,128)(2,1)S(1)}, bf16[128,1024]{1,0:T(8,128)(2,1)}, u32[]{:S(2)}) copy-start(bf16[128,1024]{1,0:T(8,128)(2,1)} %reduce-scatter.4.cloned.1.call-done) | copy-start | bytes 786436
  251.6 44.3 %all-gather.8.cloned.1.call-start = ((), (), s32[]{:S(2)}) async-start(), calls=%async_computation.7 | async-start | bytes 1310720 | tf_op jit(solution)/shard_map/all_gather | solution.py:479
  279.1 47.2 %copy-start.3 = (bf16[128,1024]{1,0:T(8,128)(2,1)S(1)}, bf16[128,1024]{1,0:T(8,128)(2,1)}, u32[]{:S(2)}) copy-start(bf16[128,1024]{1,0:T(8,128)(2,1)} %reduce-scatter.6.cloned.1.call-done) | copy-start | bytes 786436
  279.1 47.2 %reduce-scatter.8.cloned.1.call-start = ((), (), s32[]{:S(2)}) async-start(), calls=%async_computation.8 | async-start | bytes 1310720 | tf_op jit(solution)/shard_map/reduce_scatter | solution.py:482
Sparse Core Ops, SparseCore 0:
  114.9 23.4 reduce-scatter.3
  142.6 16.7 all-gather.3
  164.1 73.3 all-gather.5
  251.8 23.1 reduce-scatter.5
  279.2 16.7 all-gather.7
  301.4 24.8 reduce-scatter.7

commit v2 on v1

--- a/solution.py
+++ b/solution.py
@@ -343,163 +343,287 @@
     )(tri, image, wq, wkv)
 
 
-def project_kernel(x_ref, w_ref, *out_refs, plan, head_size):
-    width = w_ref.shape[2]
-    for j, (place, column, factor) in enumerate(plan):
-        product = jnp.dot(x_ref[...], w_ref[j], preferred_element_type=jnp.float32)
-        if factor is not None:
-            product = product * (head_scale(product, head_size) * factor)
-        out_refs[place][:, column * width : (column + 1) * width] = product.astype(jnp.bfloat16)
-
-
-def project(x, weights, plan, head_size):
-    rows, depth = x.shape
-    count, _, width = weights.shape
-    block = math.gcd(rows, 512)
-    places = max(p for p, _, _ in plan) + 1
-    widths = [width * sum(p == place for p, _, _ in plan) for place in range(places)]
+class Scatter:
+    @staticmethod
+    def scratch(heads, rows, depth):
+        pairs = heads // 2
+        dma = pltpu.SemaphoreType.DMA((pairs,))
+        tiles = [pltpu.VMEM((pairs, rows, depth), bf16)] * 3
+        return [pltpu.VMEM((pairs, 2, rows, depth), bf16)] + tiles + [dma] * 4
+
+    def __init__(self, place, refs):
+        self.place = place
+        self.part, self.close, self.sums, self.distant = refs[:4]
+        self.near_out, self.near_in, self.far_out, self.far_in = refs[4:]
+
+    def near(self, k):
+        p = self.place
+        return send(
+            self.part.at[k, 1 - p.core],
+            self.close.at[k],
+            self.near_out.at[k],
+            self.near_in.at[k],
+            p.partner(),
+        )
+
+    def far(self, k):
+        return send(
+            self.sums.at[k],
+            self.distant.at[k],
+            self.far_out.at[k],
+            self.far_in.at[k],
+            self.place.across(k),
+        )
+
+    def give(self, k, value):
+        self.part[k] = value.reshape(self.part.shape[1:]).astype(bf16)
+        self.near(k).start()
+
+    def near_sum(self, k):
+        self.near(k).wait_recv()
+        return self.part[k, self.place.core].astype(f32) + self.close[k].astype(f32)
+
+    def relay(self, k):
+        self.sums[k] = self.near_sum(k).astype(bf16)
+        self.far(k).start()
+
+    def finish(self):
+        total = self.near_sum(0)
+        for k in range(1, self.place.pairs):
+            self.far(k).wait_recv()
+            total = total + self.distant[k].astype(f32)
+        return total
+
+    def drain(self):
+        for k in range(self.place.pairs):
+            self.near(k).wait_send()
+        for k in range(1, self.place.pairs):
+            self.far(k).wait_send()
+
+
+def collect(place, scatter, mix, weight_ref):
+    both = mix.shape[0] // place.pairs
+
+    def partial(k):
+        rows = pl.ds(pl.multiple_of(place.pair_at(k) * both, both), both)
+        return dot(mix[rows, :], weight_ref[...])
+
+    for k in range(1, place.pairs):
+        scatter.give(k, partial(k))
+    scatter.give(0, partial(0))
+    for k in range(1, place.pairs):
+        scatter.relay(k)
+    return scatter.finish()
+
+
+def self_kernel(
+    tri_ref, mixed_ref, wout_ref, wqkv_ref, stream_ref, out_ref,
+    mix, chunks, column, passed, k_ref, vt_ref, acc, results, landed,
+    a_out, a_in, f_out, f_in, o_out, o_in, *refs,
+    toks, heads, head_size, factor,
+):
+    place = Place(toks, heads)
+    width, group = out_ref.shape
+    count = width // head_size
+    sharers = toks // count
+    mine, part = lax.div(place.tok, sharers), lax.rem(place.tok, sharers)
+
+    def owner(k):
+        return lax.rem(mine + k + count, count)
+
+    def owner_at(k):
+        return (owner(k) * sharers + part, place.head)
+
+    def sharer_at(m):
+        return (mine * sharers + lax.rem(part + m, sharers), place.head)
+
+    greet(
+        place.head_peers()
+        + [owner_at(k) for k in range(1, count)]
+        + [sharer_at(m) for m in range(1, sharers)]
+    )
+    scatter = Scatter(place, refs[:8])
+    gather = Gather(place, refs[8:])
+    mix[...] = jnp.transpose(mixed_ref[...].astype(f32)).astype(bf16)
+    vt_ref[head_size:, :] = jnp.ones((ONES, vt_ref.shape[1]), bf16)
+    stream = tri_ref[...].astype(f32) + collect(place, scatter, mix, wout_ref)
+    stream_ref[...] = stream
+    gather.start(layer_norm(stream).astype(bf16))
+    gather.forward()
+    gather.finish()
+    x = gather.rows[...].reshape(group, -1)
+    for j in range(3):
+        product = jnp.transpose(dot(x, wqkv_ref[j]))
+        if j < 2:
+            product = head_norm_rows(product, head_size, 1.0 if j else factor)
+        chunks[:, j * head_size : (j + 1) * head_size, :] = product.reshape(
+            count, head_size, group
+        ).astype(bf16)
+
+    def deal(k):
+        return send(
+            chunks.at[owner(k)], column.at[mine], a_out.at[k], a_in.at[k], owner_at(k)
+        )
+
+    def hand(k, m):
+        source = column.at[owner(-k), pl.ds(head_size, 2 * head_size)]
+        i = k * (sharers - 1) + m - 1
+        return send(source, passed.at[k, m - 1], f_out.at[i], f_in.at[i], sharer_at(m))
+
+    def fill(n, chunk):
+        rows = slice(n * group, (n + 1) * group)
+        k_ref[rows, :] = jnp.transpose(chunk[:head_size].astype(f32)).astype(bf16)
+        vt_ref[:head_size, rows] = chunk[head_size:]
+
+    for k in range(1, count):
+        deal(k).start()
+    column[mine] = chunks[mine]
+    for k in range(count):
+        if k:
+            deal(k).wait_recv()
+        for m in range(1, sharers):
+            hand(k, m).start()
+        fill(k, column[owner(-k), head_size:])
+
+    def give_back(j):
+        return send(results.at[j], landed.at[mine], o_out.at[j], o_in.at[j], owner_at(j + 1))
+
+    span = count * group
+    for m in range(sharers):
+        if m:
+            for k in range(count):
+                hand(k, m).wait_recv()
+                fill(m * count + k, passed[k, m - 1])
+        keys = slice(m * span, (m + 1) * span)
+        for j in range(count):
+            scores = dot(k_ref[keys, :], column[owner(j + 1), :head_size])
+            total = dot(vt_ref[:, keys], jnp.exp2(scores).astype(bf16))
+            if m:
+                total = acc[j] + total
+            if m < sharers - 1:
+                acc[j] = total
+                continue
+            result = (total[:head_size] / total[head_size : head_size + 1]).astype(bf16)
+            if j == count - 1:
+                landed[mine] = result
+            else:
+                results[j] = result
+                give_back(j).start()
+    for j in range(count - 1):
+        give_back(j).wait_recv()
+    out_ref[...] = landed[...].reshape(width, group)
+    scatter.drain()
+    gather.drain()
+    for k in range(1, count):
+        deal(k).wait_send()
+    for k in range(count):
+        for m in range(1, sharers):
+            hand(k, m).wait_send()
+    for j in range(count - 1):
+        give_back(j).wait_send()
+
+
+def self_stage(tri, mixed, wout, wqkv, toks, heads, head_size, factor):
+    rows, depth = tri.shape
+    width, group = mixed.shape
+    count = width // head_size
+    sharers = toks // count
+    vmem = pl.BlockSpec(memory_space=pltpu.VMEM)
+    dma = pltpu.SemaphoreType.DMA
+    passes = max(1, count * (sharers - 1))
     return pl.pallas_call(
-        functools.partial(project_kernel, plan=plan, head_size=head_size),
-        out_shape=[jax.ShapeDtypeStruct((rows, w), jnp.bfloat16) for w in widths],
-        grid=(rows // block,),
-        in_specs=[
-            pl.BlockSpec((block, depth), lambda i: (i, 0)),
-            pl.BlockSpec((count, depth, width), lambda i: (0, 0, 0)),
+        functools.partial(
+            self_kernel, toks=toks, heads=heads, head_size=head_size, factor=factor
+        ),
+        out_shape=[
+            jax.ShapeDtypeStruct((rows, depth), f32),
+            jax.ShapeDtypeStruct((width, group), bf16),
         ],
-        out_specs=[pl.BlockSpec((block, w), lambda i: (i, 0)) for w in widths],
-        compiler_params=pltpu.CompilerParams(vmem_limit_bytes=VMEM_LIMIT),
-        cost_estimate=pl.CostEstimate(
-            flops=2 * rows * depth * width * count,
-            bytes_accessed=2 * (rows * depth + count * depth * width + rows * width * count),
-            transcendentals=rows * width,
+        in_specs=[vmem] * 4,
+        out_specs=[vmem] * 2,
+        scratch_shapes=[
+            pltpu.VMEM((group, width), bf16),
+            pltpu.VMEM((count, 3 * head_size, group), bf16),
+            pltpu.VMEM((count, 3 * head_size, group), bf16),
+            pltpu.VMEM((count, max(1, sharers - 1), 2 * head_size, group), bf16),
+            pltpu.VMEM((toks * group, head_size), bf16),
+            pltpu.VMEM((head_size + ONES, toks * group), bf16),
+            pltpu.VMEM((count, head_size + ONES, group), f32),
+            pltpu.VMEM((count, head_size, group), bf16),
+            pltpu.VMEM((count, head_size, group), bf16),
+            dma((count,)), dma((count,)),
+            dma((passes,)), dma((passes,)),
+            dma((count,)), dma((count,)),
+        ] + Scatter.scratch(heads, rows, depth) + Gather.scratch(heads, rows, depth),
+        compiler_params=pltpu.CompilerParams(
+            vmem_limit_bytes=VMEM_LIMIT, collective_id=1, has_side_effects=True
         ),
-    )(x, weights)
-
-
-def stack_heads(queries, head_size):
-    rows, lanes = queries.shape
-    lane = lax.broadcasted_iota(jnp.int32, (rows, lanes), 1) // head_size
-    zero = jnp.zeros_like(queries)
-    heads = lanes // head_size
-    if heads == 1:
-        return queries
-    return jnp.concatenate([jnp.where(lane == h, queries, zero) for h in range(heads)], axis=0)
-
-
-def pick_heads(acc_ref, rows, lanes, head_size):
-    picked = acc_ref[:rows, :]
-    lane = lax.broadcasted_iota(jnp.int32, picked.shape, 1) % lanes // head_size
-    for h in range(1, lanes // head_size):
-        picked = jnp.where(lane == h, acc_ref[h * rows : (h + 1) * rows, :], picked)
-    return picked[:, :lanes], picked[:, lanes:]
-
-
-def fold_keys(stacked, key_of, value_of, acc_ref, key_count, lanes):
-    block = math.gcd(key_count, 512)
-    ones = jnp.ones((block, lanes), jnp.bfloat16)
-    acc_ref[...] = jnp.zeros_like(acc_ref)
-
-    def step(i, carry):
-        rows = pl.ds(pl.multiple_of(i * block, block), block)
-        scores = lax.dot_general(
-            stacked, key_of(rows), (((1,), (1,)), ((), ())), preferred_element_type=jnp.float32
-        )
-        weights = jnp.exp2(scores).astype(jnp.bfloat16)
-        values = jnp.concatenate([value_of(rows), ones], axis=1)
-        acc_ref[...] += jnp.dot(weights, values, preferred_element_type=jnp.float32)
-        return carry
-
-    lax.fori_loop(0, key_count // block, step, 0, unroll=True)
-
-
-def attend_kernel(q_ref, k_ref, v_ref, *refs, head_size, finish):
-    acc_ref = refs[-1]
-    rows, lanes = q_ref.shape
-    fold_keys(
-        stack_heads(q_ref[...], head_size),
-        lambda r: k_ref[r, :],
-        lambda r: v_ref[r, :],
-        acc_ref,
-        k_ref.shape[0],
-        lanes,
-    )
-    mixed, totals = pick_heads(acc_ref, rows, lanes, head_size)
-    if finish:
-        refs[0][...] = (mixed / totals).astype(jnp.bfloat16)
-    else:
-        refs[0][...] = mixed.astype(jnp.bfloat16)
-        refs[1][...] = totals
-
-
-def attend(queries, kv, head_size, finish):
-    count, width = queries.shape
-    keys = kv.shape[0]
-    lanes = min(128, width)
-    pairs = width // lanes
-    block = math.gcd(count, 512)
-    outs = [jax.ShapeDtypeStruct((count, width), jnp.bfloat16)]
-    if not finish:
-        outs.append(jax.ShapeDtypeStruct((count, width), jnp.float32))
-    if width % 128:
-        keys_values = (kv[:, :width], kv[:, width:])
-        shift = 0
-    else:
-        keys_values = (kv, kv)
-        shift = pairs
-    result = pl.pallas_call(
-        functools.partial(attend_kernel, head_size=head_size, finish=finish),
-        out_shape=outs,
-        grid=(pairs, count // block),
-        in_specs=[
-            pl.BlockSpec((block, lanes), lambda p, i: (i, p)),
-            pl.BlockSpec((keys, lanes), lambda p, i: (0, p)),
-            pl.BlockSpec((keys, lanes), lambda p, i: (0, p + shift)),
-        ],
-        out_specs=[pl.BlockSpec((block, lanes), lambda p, i: (i, p))] * len(outs),
-        scratch_shapes=[pltpu.VMEM((lanes // head_size * block, 2 * lanes), jnp.float32)],
-        compiler_params=pltpu.CompilerParams(vmem_limit_bytes=VMEM_LIMIT),
-        cost_estimate=pl.CostEstimate(
-            flops=16 * count * keys * width,
-            bytes_accessed=2 * (3 * count * width + 2 * keys * width),
-            transcendentals=count * keys * width // head_size,
+        name="self_stage",
+    )(tri, mixed, wout, wqkv)
+
+
+def mlp_kernel(
+    stream_ref, mixed_ref, wout_ref, win_ref, wdown_ref, out_ref, mix, *refs, toks, heads
+):
+    place = Place(toks, heads)
+    greet(place.head_peers())
+    scatter = Scatter(place, refs[:8])
+    second = Scatter(place, refs[8:16])
+    gather = Gather(place, refs[16:])
+    mix[...] = jnp.transpose(mixed_ref[...].astype(f32)).astype(bf16)
+    stream = stream_ref[...] + collect(place, scatter, mix, wout_ref)
+    gather.start(layer_norm(stream).astype(bf16))
+
+    def mlp(k):
+        x = gather.rows[pl.ds(place.pair_at(k) * 2, 2)].reshape(-1, stream.shape[1])
+        hidden = jax.nn.gelu(dot(x, win_ref[...]), approximate=True).astype(bf16)
+        second.give(k, dot(hidden, wdown_ref[...]))
+
+    gather.near_arrival(0).wait_recv()
+    mlp(0)
+    gather.forward()
+    for k in range(1, place.pairs):
+        gather.near_arrival(k).wait_recv()
+    for k in range(1, place.pairs):
+        mlp(k)
+    for k in range(1, place.pairs):
+        second.relay(k)
+    out_ref[...] = (stream + second.finish()).astype(bf16)
+    scatter.drain()
+    second.drain()
+    gather.drain()
+
+
+def mlp_stage(stream, mixed, wout, win, wdown, toks, heads):
+    rows, depth = stream.shape
+    width, group = mixed.shape
+    vmem = pl.BlockSpec(memory_space=pltpu.VMEM)
+    return pl.pallas_call(
+        functools.partial(mlp_kernel, toks=toks, heads=heads),
+        out_shape=jax.ShapeDtypeStruct((rows, depth), bf16),
+        in_specs=[vmem] * 5,
+        out_specs=vmem,
+        scratch_shapes=[pltpu.VMEM((group, width), bf16)]
+        + Scatter.scratch(heads, rows, depth) * 2
+        + Gather.scratch(heads, rows, depth),
+        compiler_params=pltpu.CompilerParams(
+            vmem_limit_bytes=VMEM_LIMIT, collective_id=2, has_side_effects=True
         ),
-    )(queries, *keys_values)
-    return result
+        name="mlp_stage",
+    )(stream, mixed, wout, win, wdown)
 
 
 def per_device(
     tri_tokens, image_tokens, cross_q, cross_kv, cross_out, self_qkv, self_out, mlp_in, mlp_out,
     *, tok, head
 ):
-    width = cross_q.shape[1]
     head_size = tri_tokens.shape[1] // HEADS
-    query_factor = score_gain / math.sqrt(head_size) * math.log2(math.e)
-
-    def spread(stream):
-        return lax.all_gather(layer_norm(stream).astype(jnp.bfloat16), "head", axis=0, tiled=True)
-
-    def collect(operand, weight):
-        return lax.psum_scatter(
-            jnp.dot(operand, weight, preferred_element_type=jnp.float32).astype(jnp.bfloat16),
-            "head",
-            scatter_dimension=0,
-            tiled=True,
-        ).astype(jnp.float32)
-
-    stream_zero = tri_tokens.astype(jnp.float32)
-    mixed = cross(tri_tokens, image_tokens, cross_q, cross_kv, tok, head, head_size, query_factor)
-    mix = mixed.T
-    stream_one = stream_zero + collect(mix, cross_out)
-    self_queries, self_kv = project(
-        spread(stream_one), self_qkv, ((0, 0, query_factor), (1, 0, 1.0), (1, 1, None)), head_size
+    factor = score_gain / math.sqrt(head_size) * math.log2(math.e)
+    mixed = cross(tri_tokens, image_tokens, cross_q, cross_kv, tok, head, head_size, factor)
+    stream, mixed = self_stage(
+        tri_tokens, mixed, cross_out, self_qkv, tok, head, head_size, factor
     )
-    all_kv = lax.all_gather(self_kv, "tok", axis=0, tiled=True)
-    (mix,) = attend(self_queries, all_kv, head_size, True)
-    stream_two = stream_one + collect(mix, self_out)
-    hidden = jax.nn.gelu(
-        jnp.dot(spread(stream_two), mlp_in, preferred_element_type=jnp.float32), approximate=True
-    ).astype(jnp.bfloat16)
-    return (stream_two + collect(hidden, mlp_out)).astype(jnp.bfloat16)
+    return mlp_stage(stream, mixed, self_out, mlp_in, mlp_out, tok, head)
 
 
 def solution(mesh):

time: 335 us -> 200 us (0.60)
  waiting for transfers between devices: 179 us -> 0 us
  Pallas kernels: 122 us -> 198 us
  between operations: 13.5 us -> 0.03 us
  matrix products: 10.1 us -> 0 us
  other arithmetic: 9.98 us -> 0 us
    all_gather x3 -> x0, waiting for transfers between devices: 107 us -> none  [the longest x1 73.3 us: per_device(): all_kv = lax.all_gather(self_kv, 'tok', axis=0, tiled=True)]
    pallas_call x2, Pallas kernels: 16.3 us -> 92.2 us  [the longest x1 59.7 us: self_stage(): pl.pallas_call(functools.partial(self_kernel, toks=toks, heads=heads, hea...]
    reduce_scatter x3 -> x0, waiting for transfers between devices: 71.9 us -> none  [collect(): lax.psum_scatter(jnp.dot(operand, weight, preferred_element_type=jnp.floa...]
    dot_general x3 -> x0, matrix products: 10.1 us -> none  [collect(): jnp.dot(operand, weight, preferred_element_type=jnp.float32)]
    convert_element_type x3 -> x0, other arithmetic: 5.4 us -> none  [the longest x2 3.58 us: spread(): layer_norm(stream).astype(jnp.bfloat16)]
    reduce_sum x4 -> x0, other arithmetic: 4.55 us -> none  [the longest x2 2.32 us: layer_norm(): jnp.mean(centered * centered, axis=-1, keepdims=True) + 1e-05]
  transfers between devices with their start and end apart: 6 -> 0, of which waited for: 6 -> 0; matrix products, arithmetic and copies ran while one was open for 0% -> 0% of each run, Pallas kernels for 0% -> 0%
where the time goes in v2:
time: 200 us
  Pallas kernels  198 us (99%)
    pallas_call x1, Pallas kernels, cross(): pl.pallas_call(functools.partial(cross_kernel, toks=toks, heads=heads, he...  106 us
    pallas_call x1, Pallas kernels, self_stage(): pl.pallas_call(functools.partial(self_kernel, toks=toks, heads=heads, hea...  59.7 us
    pallas_call x1, Pallas kernels, mlp_stage(): pl.pallas_call(functools.partial(mlp_kernel, toks=toks, heads=heads), out...  32.5 us

profile of v2, /device:TPU:0, one launch (start us, length us, event | category | flops | bytes accessed | tf_op | source)
XLA Modules:
  0.0 199.5 jit_solution(15916217150632267965)
XLA Ops:
  0.0 105.6 %cross.1.mixed_ref = bf16[256,512]{1,0:T(8,128)(2,1)} custom-call(bf16[128,1024]{1,0:T(8,128)(2,1)} %tri_ref.3, bf16[4096,1024]{1,0:T(8,128)(2,1)} %image_ref.1, bf16[1024,256]{1,0:T(8,128)(2,1)} %wq_ref.1, bf16[2,1024,256]{2,1,0:T(8,128)(2,1)} %wkv_ref.1), custom_call_target="tpu_custom_call" | custom-call | tf_op jit(solution)/shard_map/cross/pallas_call | solution.py:317
  105.6 59.7 %self_stage.1 = (f32[128,1024]{1,0:T(8,128)}, bf16[256,512]{1,0:T(8,128)(2,1)}) custom-call(bf16[128,1024]{1,0:T(8,128)(2,1)} %tri_ref.3, bf16[256,512]{1,0:T(8,128)(2,1)} %cross.1.mixed_ref, bf16[256,1024]{1,0:T(8,128)(2,1)} %wout_ref.2, bf16[3,1024,256]{2,1,0:T(8,128)(2,1)} %wqkv_ref.1), custom_call_target="tpu_custom_call" | custom-call | tf_op jit(solution)/shard_map/self_stage/pallas_call | solution.py:534
  165.4 32.5 %mlp_stage.1 = bf16[128,1024]{1,0:T(8,128)(2,1)} custom-call(f32[128,1024]{1,0:T(8,128)} %get-tuple-element.7.stream_ref, bf16[256,512]{1,0:T(8,128)(2,1)} %get-tuple-element.8.mixed_ref, bf16[256,1024]{1,0:T(8,128)(2,1)} %wout_ref.3, bf16[1024,1024]{1,0:T(8,128)(2,1)} %win_ref.1, bf16[1024,1024]{1,0:T(8,128)(2,1)} %wdown_ref.1), custom_call_target="tpu_custom_call" | custom-call | tf_op jit(solution)/shard_map/mlp_stage/pallas_call | solution.py:601
  197.9 1.7 copy.11

commit v3 on v2

--- a/solution.py
+++ b/solution.py
@@ -13,6 +13,8 @@
 VMEM_LIMIT = 60 << 20
 MESH = pl.DeviceIdType.MESH
 ONES = 16
+FORWARD_AT = 2
+QUERY_AT = 3
 bf16 = jnp.bfloat16
 f32 = jnp.float32
 
@@ -169,15 +171,104 @@
     return pack(jnp.concatenate(mixed, axis=0), totals[:8])
 
 
+class Share:
+    @staticmethod
+    def scratch(count, heads):
+        dma = pltpu.SemaphoreType.DMA((count * (heads // 2),))
+        return [dma, dma, dma, dma, pltpu.SemaphoreType.DMA((count,))]
+
+    def __init__(self, place, own, full, sems):
+        self.place, self.own, self.full = place, own, full
+        self.far_out, self.far_in, self.near_out, self.near_in, self.local_sem = sems
+
+    def far(self, i, k):
+        p = self.place
+        n = i * p.pairs + k
+        return send(
+            self.own[i], self.full[i](p.head), self.far_out.at[n], self.far_in.at[n], p.across(k)
+        )
+
+    def near(self, i, k):
+        p = self.place
+        n = i * p.pairs + k
+        slot = self.full[i](p.pair_at(-k) * 2 + p.core)
+        source = slot if k else self.own[i]
+        return send(source, slot, self.near_out.at[n], self.near_in.at[n], p.partner())
+
+    def local(self, i):
+        return pltpu.make_async_copy(
+            self.own[i], self.full[i](self.place.head), self.local_sem.at[i]
+        )
+
+    def start(self, i):
+        for k in range(1, self.place.pairs):
+            self.far(i, k).start()
+        self.near(i, 0).start()
+        self.local(i).start()
+
+    def forward(self, i):
+        for k in range(1, self.place.pairs):
+            self.far(i, k).wait_recv()
+            self.near(i, k).start()
+
+    def finish(self, i):
+        self.local(i).wait()
+        for k in range(self.place.pairs):
+            self.near(i, k).wait()
+        for k in range(1, self.place.pairs):
+            self.far(i, k).wait_send()
+
+
+def pick(step, values):
+    chosen = jnp.int32(values[0])
+    for i, value in enumerate(values):
+        chosen = jnp.where(step == i, jnp.int32(value), chosen)
+    return chosen
+
+
+def block_order(lines):
+    order = sorted(range(1, lines), key=lambda k: (-min(k, lines - k), k))
+    turns = [(False, lines)]
+    for k in order[:-1]:
+        turns += [(True, k), (False, k)]
+    for k in order[-1:]:
+        turns += [(False, k), (True, k)]
+    turns.append((True, lines))
+    take, combine = {}, {}
+    for j, k in enumerate(order):
+        if j == 0:
+            take.setdefault(0, []).append(k)
+        elif j == len(order) - 1:
+            take.setdefault(turns.index((False, order[j - 1])), []).append(k)
+        else:
+            take.setdefault(turns.index((True, k)), []).append(k)
+        after = turns.index((True, k)) if j == len(order) - 1 else turns.index((False, k)) + 1
+        combine.setdefault(after, []).append(k)
+    return order, turns, take, combine
+
+
 def cross_kernel(
-    tri_ref, image_ref, wq_ref, wkv_ref, out_ref,
+    tri_ref, image_ref, wq_ref, wkv_ref, *rest,
+    toks, heads, head_size, factor, shared,
+):
+    own_refs, out_ref, full_refs = rest[:shared], rest[shared], rest[shared + 1 : 2 * shared + 1]
+    cross_body(
+        tri_ref, image_ref, wq_ref, wkv_ref, own_refs, out_ref, full_refs,
+        *rest[2 * shared + 1 :], toks=toks, heads=heads, head_size=head_size, factor=factor,
+    )
+
+
+def cross_body(
+    tri_ref, image_ref, wq_ref, wkv_ref, own_refs, out_ref, full_refs,
     image, k_ref, vt_ref, queries, tiles, pair_tiles, joined, far_tiles,
-    image_sem, q_out, q_in, f_out, f_in, p_out, p_in, c_out, c_in, *gather_refs,
+    image_sem, q_out, q_in, f_out, f_in, p_out, p_in, c_out, c_in, *refs,
     toks, heads, head_size, factor,
 ):
     place = Place(toks, heads)
-    width, group = out_ref.shape
+    _, width, rows_each = out_ref.shape
+    group = rows_each * heads
     lines = toks // 2
+    order, turns, take, combine = block_order(lines)
     line, side = lax.div(place.tok, 2), lax.rem(place.tok, 2)
     neighbour = (line * 2 + 1 - side, place.head)
 
@@ -198,7 +289,13 @@
     for i in range(steps):
         fetch(i).start()
     greet(place.head_peers() + [neighbour] + [peer(k) for k in range(1, lines)])
-    gather = Gather(place, gather_refs)
+    gather = Gather(place, refs[:5])
+    own, full = [], []
+    for mine, whole in zip(own_refs, full_refs):
+        for j in range(mine.shape[0]):
+            own.append(mine.at[j])
+            full.append(functools.partial(lambda slot, whole, j: whole.at[slot, j], whole=whole, j=j))
+    share = Share(place, own, full, refs[5:]) if own else None
     gather.start(layer_norm(tri_ref[...].astype(f32)).astype(bf16))
     vt_ref[:, head_size:, :] = jnp.ones((width // head_size, ONES, keys), bf16)
 
@@ -211,18 +308,21 @@
         return send(slot, slot, q_out.at[k], q_in.at[k], peer(k))
 
     def project(i, carry):
-        @pl.when(i == steps // 2)
+        @pl.when(i == FORWARD_AT * steps // 8)
         def _():
             gather.forward()
 
-        @pl.when(i == steps * 3 // 4)
+        @pl.when(i == QUERY_AT * steps // 8)
         def _():
             gather.finish()
             x = gather.rows[...].reshape(group, -1)
             product = jnp.transpose(dot(x, wq_ref[...]))
             queries[place.tok] = head_norm_rows(product, head_size, factor).astype(bf16)
-            if lines > 1:
-                q_send(1).start()
+            q_send(0).start()
+            for k in order:
+                q_send(k).start()
+            for n in range(min(2, len(own))):
+                share.start(n)
 
         rows = pl.ds(pl.multiple_of(i * step_rows, step_rows), step_rows)
         fetch(i).wait()
@@ -234,10 +334,6 @@
         return carry
 
     lax.fori_loop(0, steps, project, 0)
-    for k in range(2, lines):
-        q_send(k).start()
-    q_send(0).start()
-
     def forward(k, slot):
         block = queries.at[slot]
         return send(block, block, f_out.at[k], f_in.at[k], neighbour)
@@ -248,44 +344,56 @@
     def far_send(k):
         return send(joined.at[k], far_tiles.at[k], c_out.at[k], c_in.at[k], peer(k))
 
+    def turn_of(n):
+        return min(len(turns) - 2, max(0, n - 3))
+
+    def arrive(k):
+        slot = lax.rem(line + k, lines) * 2 + side
+        block = queries.at[slot]
+        send(block, block, q_out.at[k], q_in.at[k], neighbour).wait_recv()
+        forward(k, slot).start()
+
+    def before(i):
+        mine, k = turns[i]
+        if not mine and k == lines:
+            block = queries.at[line * 2 + 1 - side]
+            send(block, block, q_out.at[0], q_in.at[0], neighbour).wait_recv()
+        for taken in take.get(i, []):
+            arrive(taken)
+        if not mine and k < lines:
+            forward(k, lax.rem(line + k, lines) * 2 + 1 - side).wait_recv()
+        if own:
+            for n in range(2, len(own)):
+                if i == turn_of(n):
+                    share.start(n)
+
+    def after(i):
+        mine, k = turns[i]
+        if not mine:
+            pair_send(k, i).start()
+        for done in combine.get(i, []):
+            pair_send(done, i).wait_recv()
+            joined[done] = pack(
+                *join([tiles[turns.index((True, done))], pair_tiles[done]], width)
+            )
+            far_send(done).start()
+        if own:
+            for n in range(len(own)):
+                if i == min(len(turns) - 1, turn_of(n) + 1):
+                    share.forward(n)
+
     def attend(s, carry):
-        k = lax.div(s, 2) + 1
-        last = k == lines
-        first = lax.rem(s, 2) == 0
-        mine = first != last
-        slot = lax.rem(line + k, lines) * 2 + jnp.where(mine, side, 1 - side)
-
-        @pl.when(jnp.logical_and(first, jnp.logical_not(last)))
-        def _():
-            block = queries.at[slot]
-            send(block, block, q_out.at[k], q_in.at[k], neighbour).wait_recv()
-            forward(k, slot).start()
-
-        @pl.when(jnp.logical_and(jnp.logical_not(first), jnp.logical_not(last)))
-        def _():
-            forward(k, slot).wait_recv()
-
-        @pl.when(jnp.logical_and(first, last))
-        def _():
-            block = queries.at[slot]
-            send(block, block, q_out.at[0], q_in.at[0], neighbour).wait_recv()
-
+        for i in range(len(turns)):
+            pl.when(s == i)(functools.partial(before, i))
+        k = pick(s, [k for _, k in turns])
+        mine = pick(s, [int(m) for m, _ in turns])
+        slot = lax.rem(line + k, lines) * 2 + mine * side + (1 - mine) * (1 - side)
         tiles[s] = attend_block(queries[slot], k_ref, vt_ref, head_size)
-
-        @pl.when(jnp.logical_not(mine))
-        def _():
-            pair_send(k, s).start()
-
-        @pl.when(jnp.logical_and(first, k > 1))
-        def _():
-            before = k - 1
-            pair_send(before, s).wait_recv()
-            joined[before] = pack(*join([tiles[2 * before - 2], pair_tiles[before]], width))
-            far_send(before).start()
-
+        for i in range(len(turns)):
+            pl.when(s == i)(functools.partial(after, i))
         return carry
 
-    lax.fori_loop(0, 2 * lines, attend, 0)
+    lax.fori_loop(0, len(turns), attend, 0)
     pair_send(lines, 0).wait_recv()
     for k in range(1, lines):
         far_send(k).wait_recv()
@@ -294,7 +402,9 @@
     )
     for h in range(width // head_size):
         rows = slice(h * head_size, (h + 1) * head_size)
-        out_ref[rows, :] = (mixed[rows] / totals[h : h + 1]).astype(bf16)
+        mix = (mixed[rows] / totals[h : h + 1]).astype(bf16)
+        for n in range(heads):
+            out_ref[n, rows, :] = mix[:, n * rows_each : (n + 1) * rows_each]
     gather.drain()
     for k in range(lines):
         q_send(k).wait_send()
@@ -303,9 +413,11 @@
         far_send(k).wait_send()
     for k in range(1, lines + 1):
         pair_send(k, 0).wait_send()
-
-
-def cross(tri, image, wq, wkv, toks, heads, head_size, factor):
+    for n in range(len(own)):
+        share.finish(n)
+
+
+def cross(tri, image, wq, wkv, weights, toks, heads, head_size, factor):
     rows, depth = tri.shape
     keys = image.shape[0]
     width = wq.shape[1]
@@ -313,14 +425,18 @@
     lines = toks // 2
     tile = (width + 16, group)
     vmem = pl.BlockSpec(memory_space=pltpu.VMEM)
+    anywhere = pl.BlockSpec(memory_space=pl.ANY)
+    pieces = sum(w.shape[0] for w in weights)
     dma = pltpu.SemaphoreType.DMA
     return pl.pallas_call(
         functools.partial(
-            cross_kernel, toks=toks, heads=heads, head_size=head_size, factor=factor
+            cross_kernel, toks=toks, heads=heads, head_size=head_size, factor=factor,
+            shared=len(weights),
         ),
-        out_shape=jax.ShapeDtypeStruct((width, group), bf16),
-        in_specs=[vmem, pl.BlockSpec(memory_space=pl.ANY), vmem, vmem],
-        out_specs=vmem,
+        out_shape=[jax.ShapeDtypeStruct((heads, width, rows), bf16)]
+        + [jax.ShapeDtypeStruct((heads,) + w.shape, bf16) for w in weights],
+        in_specs=[vmem, anywhere, vmem, vmem] + [anywhere] * len(weights),
+        out_specs=[vmem] + [anywhere] * len(weights),
         scratch_shapes=[
             pltpu.VMEM((keys, depth), bf16),
             pltpu.VMEM((keys, width), bf16),
@@ -335,12 +451,14 @@
             dma((lines,)), dma((lines,)),
             dma((lines + 1,)), dma((lines + 1,)),
             dma((lines,)), dma((lines,)),
-        ] + Gather.scratch(heads, rows, depth),
+        ]
+        + Gather.scratch(heads, rows, depth)
+        + (Share.scratch(pieces, heads) if weights else []),
         compiler_params=pltpu.CompilerParams(
             vmem_limit_bytes=VMEM_LIMIT, collective_id=0, has_side_effects=True
         ),
         name="cross",
-    )(tri, image, wq, wkv)
+    )(tri, image, wq, wkv, *weights)
 
 
 class Scatter:
@@ -613,13 +731,254 @@
     )(stream, mixed, wout, win, wdown)
 
 
+def late_kernel(
+    tri_ref, mixed_ref, cross_out_ref, qkv_ref, self_out_ref, win_ref, wdown_ref, out_ref,
+    cross_out, qkv, self_out, win, down, mixes, chunks, column, passed, k_ref, vt_ref, acc,
+    results, landed, load_sem, m_out, m_in, a_out, a_in, f_out, f_in, r_out, r_in, *refs,
+    toks, heads, head_size, factor,
+):
+    place = Place(toks, heads)
+    rows, depth = tri_ref.shape
+    width = mixed_ref.shape[1]
+    count = width // head_size
+    sharers = toks // count
+    sources = count * heads
+    mine, part = lax.div(place.tok, sharers), lax.rem(place.tok, sharers)
+    every = [(a, h) for h in range(heads) for a in range(count)]
+
+    def owner(a):
+        return lax.rem(mine + a + count, count)
+
+    def column_at(h):
+        return lax.rem(place.head + h + heads, heads)
+
+    def device_at(a, h):
+        return (owner(a) * sharers + part, column_at(h))
+
+    def sharer_at(m):
+        return (mine * sharers + lax.rem(part + m, sharers), place.head)
+
+    def load(i):
+        source, target = [
+            (cross_out_ref, cross_out), (qkv_ref, qkv), (self_out_ref, self_out),
+            (win_ref, win), (wdown_ref, down),
+        ][i]
+        return pltpu.make_async_copy(source, target, load_sem.at[i])
+
+    for i in range(5):
+        load(i).start()
+    greet(
+        [device_at(a, h) for a, h in every if (a, h) != (0, 0)]
+        + [sharer_at(m) for m in range(1, sharers)]
+    )
+    scatter = Scatter(place, refs[:8])
+    gather = Gather(place, refs[8:])
+
+    def swap(h):
+        return send(
+            mixed_ref.at[column_at(h)], mixes.at[place.head], m_out.at[h], m_in.at[h],
+            device_at(0, h),
+        )
+
+    for h in range(1, heads):
+        swap(h).start()
+    mixes[place.head] = mixed_ref[place.head]
+    vt_ref[head_size:, :] = jnp.ones((ONES, vt_ref.shape[1]), bf16)
+    load(0).wait()
+    for h in range(1, heads):
+        swap(h).wait_recv()
+
+    def turned(ref):
+        return jnp.transpose(ref[...].reshape(-1, rows).astype(f32)).astype(bf16)
+
+    stream = tri_ref[...].astype(f32) + dot(turned(mixes), cross_out[...].reshape(-1, depth))
+    x = layer_norm(stream).astype(bf16)
+    load(1).wait()
+
+    def deal(a, h):
+        i = a * heads + h
+        return send(
+            chunks.at[column_at(h), owner(a)],
+            column.at[mine * heads + place.head],
+            a_out.at[i], a_in.at[i], device_at(a, h),
+        )
+
+    def project(h):
+        n = column_at(h)
+        for j in range(3):
+            product = jnp.transpose(dot(x, qkv[n, j]))
+            if j < 2:
+                product = head_norm_rows(product, head_size, 1.0 if j else factor)
+            chunks[n, :, j * head_size : (j + 1) * head_size, :] = product.reshape(
+                count, head_size, rows
+            ).astype(bf16)
+
+    for h in range(heads):
+        project(h)
+        for a in sorted(range(count), key=lambda a: -min(a, count - a)):
+            if (a, h) != (0, 0):
+                deal(a, h).start()
+    column[mine * heads + place.head] = chunks[place.head, mine]
+
+    def slot_of(a, h):
+        return owner(-a) * heads + column_at(-h)
+
+    def hand(i, m):
+        a, h = every[i]
+        n = (m - 1) * sources + i
+        source = column.at[slot_of(a, h), pl.ds(head_size, 2 * head_size)]
+        return send(source, passed.at[m - 1, i], f_out.at[n], f_in.at[n], sharer_at(m))
+
+    def fill(n, chunk):
+        keys = slice(n * rows, (n + 1) * rows)
+        k_ref[keys, :] = jnp.transpose(chunk[:head_size].astype(f32)).astype(bf16)
+        vt_ref[:head_size, keys] = chunk[head_size:]
+
+    for i, (a, h) in enumerate(every):
+        if (a, h) != (0, 0):
+            deal(a, h).wait_recv()
+        for m in range(1, sharers):
+            hand(i, m).start()
+        fill(i, column[slot_of(a, h), head_size:])
+
+    def give_back(a, h):
+        i = a * heads + h
+        return send(
+            results.at[a, column_at(h)],
+            landed.at[place.head * count + mine],
+            r_out.at[i], r_in.at[i], device_at(a, h),
+        )
+
+    span = sources * rows
+    blocks = [(j + 1) % count for j in range(count)]
+    for m in range(sharers):
+        if m:
+            for i in range(sources):
+                hand(i, m).wait_recv()
+                fill(m * sources + i, passed[m - 1, i])
+        keys = slice(m * span, (m + 1) * span)
+        for a in blocks:
+            queries = jnp.concatenate(
+                [column[owner(a) * heads + n, :head_size] for n in range(heads)], axis=1
+            )
+            scores = dot(k_ref[keys, :], queries)
+            total = dot(vt_ref[:, keys], jnp.exp2(scores).astype(bf16))
+            if m:
+                total = acc[a] + total
+            if m < sharers - 1:
+                acc[a] = total
+                continue
+            result = (total[:head_size] / total[head_size : head_size + 1]).astype(bf16)
+            for n in range(heads):
+                results[a, n] = result[:, n * rows : (n + 1) * rows]
+            for h in range(heads):
+                if (a, h) != (0, 0):
+                    give_back(a, h).start()
+    landed[place.head * count + mine] = results[0, place.head]
+    for i in range(2, 5):
+        load(i).wait()
+    for a, h in every:
+        if (a, h) != (0, 0):
+            give_back(a, h).wait_recv()
+    stream = stream + dot(turned(landed), self_out[...].reshape(-1, depth))
+    gather.start(layer_norm(stream).astype(bf16))
+
+    def mlp(k):
+        x = gather.rows[pl.ds(place.pair_at(k) * 2, 2)].reshape(-1, depth)
+        hidden = jax.nn.gelu(dot(x, win[...]), approximate=True).astype(bf16)
+        scatter.give(k, dot(hidden, down[...]))
+
+    gather.near_arrival(0).wait_recv()
+    mlp(0)
+    gather.forward()
+    for k in range(1, place.pairs):
+        gather.near_arrival(k).wait_recv()
+    for k in range(1, place.pairs):
+        mlp(k)
+    for k in range(1, place.pairs):
+        scatter.relay(k)
+    out_ref[...] = (stream + scatter.finish()).astype(bf16)
+    scatter.drain()
+    gather.drain()
+    for h in range(1, heads):
+        swap(h).wait_send()
+    for a, h in every:
+        if (a, h) != (0, 0):
+            deal(a, h).wait_send()
+            give_back(a, h).wait_send()
+    for i in range(sources):
+        for m in range(1, sharers):
+            hand(i, m).wait_send()
+
+
+def late_stage(tri, mixed, cross_out, qkv, self_out, win, wdown, toks, heads, head_size, factor):
+    rows, depth = tri.shape
+    width = mixed.shape[1]
+    count = width // head_size
+    sharers = toks // count
+    sources = count * heads
+    vmem = pl.BlockSpec(memory_space=pltpu.VMEM)
+    anywhere = pl.BlockSpec(memory_space=pl.ANY)
+    dma = pltpu.SemaphoreType.DMA
+    passes = max(1, sources * (sharers - 1))
+    return pl.pallas_call(
+        functools.partial(
+            late_kernel, toks=toks, heads=heads, head_size=head_size, factor=factor
+        ),
+        out_shape=jax.ShapeDtypeStruct((rows, depth), bf16),
+        in_specs=[vmem] * 2 + [anywhere] * 5,
+        out_specs=vmem,
+        scratch_shapes=[
+            pltpu.VMEM(cross_out.shape, bf16),
+            pltpu.VMEM(qkv.shape, bf16),
+            pltpu.VMEM(self_out.shape, bf16),
+            pltpu.VMEM(win.shape, bf16),
+            pltpu.VMEM(wdown.shape, bf16),
+            pltpu.VMEM((heads, width, rows), bf16),
+            pltpu.VMEM((heads, count, 3 * head_size, rows), bf16),
+            pltpu.VMEM((sources, 3 * head_size, rows), bf16),
+            pltpu.VMEM((max(1, sharers - 1), sources, 2 * head_size, rows), bf16),
+            pltpu.VMEM((toks * heads * rows, head_size), bf16),
+            pltpu.VMEM((head_size + ONES, toks * heads * rows), bf16),
+            pltpu.VMEM((count, head_size + ONES, heads * rows), f32),
+            pltpu.VMEM((count, heads, head_size, rows), bf16),
+            pltpu.VMEM((sources, head_size, rows), bf16),
+            dma((5,)), dma((heads,)), dma((heads,)),
+            dma((sources,)), dma((sources,)),
+            dma((passes,)), dma((passes,)),
+            dma((sources,)), dma((sources,)),
+        ] + Scatter.scratch(heads, rows, depth) + Gather.scratch(heads, rows, depth),
+        compiler_params=pltpu.CompilerParams(
+            vmem_limit_bytes=VMEM_LIMIT, collective_id=3, has_side_effects=True
+        ),
+        name="late_stage",
+    )(tri, mixed, cross_out, qkv, self_out, win, wdown)
+
+
 def per_device(
     tri_tokens, image_tokens, cross_q, cross_kv, cross_out, self_qkv, self_out, mlp_in, mlp_out,
     *, tok, head
 ):
-    head_size = tri_tokens.shape[1] // HEADS
+    rows, depth = tri_tokens.shape
+    head_size = depth // HEADS
     factor = score_gain / math.sqrt(head_size) * math.log2(math.e)
-    mixed = cross(tri_tokens, image_tokens, cross_q, cross_kv, tok, head, head_size, factor)
+    width = cross_q.shape[1]
+    weights = []
+    if rows % 128 == 0:
+        weights = [
+            cross_out.reshape(2, -1, depth),
+            self_qkv.reshape(6, -1, width),
+            self_out.reshape(2, -1, depth),
+        ]
+    mixed, *weights = cross(
+        tri_tokens, image_tokens, cross_q, cross_kv, weights, tok, head, head_size, factor
+    )
+    if weights:
+        weights[1] = weights[1].reshape(head, 3, depth, width)
+        return late_stage(
+            tri_tokens, mixed, *weights, mlp_in, mlp_out, tok, head, head_size, factor
+        )
+    mixed = mixed.transpose(1, 0, 2).reshape(mixed.shape[1], -1)
     stream, mixed = self_stage(
         tri_tokens, mixed, cross_out, self_qkv, tok, head, head_size, factor
     )

time: 200 us -> 171 us (0.85)
  Pallas kernels: 198 us -> 169 us
    pallas_call x2 -> x1, Pallas kernels: 92.2 us -> 67.7 us  [late_stage(): pl.pallas_call(functools.partial(late_kernel, toks=toks, heads=heads, hea...]
    pallas_call x1, Pallas kernels: 106 us -> 101 us  [cross(): pl.pallas_call(functools.partial(cross_kernel, toks=toks, heads=heads, he...]
where the time goes in v3:
time: 171 us
  Pallas kernels  169 us (99%)
    pallas_call x1, Pallas kernels, cross(): pl.pallas_call(functools.partial(cross_kernel, toks=toks, heads=heads, he...  101 us
    pallas_call x1, Pallas kernels, late_stage(): pl.pallas_call(functools.partial(late_kernel, toks=toks, heads=heads, hea...  67.7 us

profile of v3, /device:TPU:0, one launch (start us, length us, event | category | flops | bytes accessed | tf_op | source)
XLA Modules:
  0.0 170.5 jit_solution(14198423827856036704)
XLA Ops:
  0.0 101.1 %cross.1 = (bf16[4,256,128]{2,1,0:T(8,128)(2,1)}, bf16[4,2,128,1024]{3,2,1,0:T(8,128)(2,1)}, bf16[4,6,512,256]{3,2,1,0:T(8,128)(2,1)}, bf16[4,2,128,1024]{3,2,1,0:T(8,128)(2,1)}) custom-call(bf16[128,1024]{1,0:T(8,128)(2,1)} %tri_ref.3, bf16[4096,1024]{1,0:T(8,128)(2,1)} %image_ref.1, bf16[1024,256]{1,0:T(8,128)(2,1)} %wq_ref.1, ...), custom_call_target="tpu_custom_call" | custom-call | tf_op jit(solution)/shard_map/cross/pallas_call | solution.py:431
  101.1 67.7 %late_stage.1 = bf16[128,1024]{1,0:T(8,128)(2,1)} custom-call(bf16[128,1024]{1,0:T(8,128)(2,1)} %tri_ref.3, bf16[4,256,128]{2,1,0:T(8,128)(2,1)} %get-tuple-element.9.mixed_ref, bf16[4,2,128,1024]{3,2,1,0:T(8,128)(2,1)} %get-tuple-element.10.cross_out_ref, bf16[4,3,1024,256]{3,2,1,0:T(8,128)(2,1)} %bitcast.4, ...), custom_call_target="tpu_custom_call" | custom-call | tf_op jit(solution)/shard_map/late_stage/pallas_call | solution.py:924
  168.9 1.7 copy.11

commit v4 on v3

--- a/solution.py
+++ b/solution.py
@@ -15,6 +15,8 @@
 ONES = 16
 FORWARD_AT = 2
 QUERY_AT = 3
+LAG = 2
+STEP = 512
 bf16 = jnp.bfloat16
 f32 = jnp.float32
 
@@ -236,14 +238,11 @@
     turns.append((True, lines))
     take, combine = {}, {}
     for j, k in enumerate(order):
-        if j == 0:
-            take.setdefault(0, []).append(k)
-        elif j == len(order) - 1:
-            take.setdefault(turns.index((False, order[j - 1])), []).append(k)
-        else:
-            take.setdefault(turns.index((True, k)), []).append(k)
-        after = turns.index((True, k)) if j == len(order) - 1 else turns.index((False, k)) + 1
-        combine.setdefault(after, []).append(k)
+        early = j + 1 if j < 3 else 2 * j - 1
+        take.setdefault(min(early, min(turns.index((m, k)) for m in (True, False))), []).append(k)
+        last = j == len(order) - 1
+        after = turns.index((True, k)) if last else turns.index((False, k)) + LAG
+        combine.setdefault(min(after, len(turns) - (2 if last else 3)), []).append(k)
     return order, turns, take, combine
 
 
@@ -279,7 +278,7 @@
         return (line_at(k) * 2 + side, place.head)
 
     keys = k_ref.shape[0]
-    step_rows = math.gcd(keys, 512)
+    step_rows = math.gcd(keys, STEP)
     steps = keys // step_rows
 
     def fetch(i):
@@ -319,7 +318,7 @@
             product = jnp.transpose(dot(x, wq_ref[...]))
             queries[place.tok] = head_norm_rows(product, head_size, factor).astype(bf16)
             q_send(0).start()
-            for k in order:
+            for k in order[:1]:
                 q_send(k).start()
             for n in range(min(2, len(own))):
                 share.start(n)
@@ -358,6 +357,9 @@
         if not mine and k == lines:
             block = queries.at[line * 2 + 1 - side]
             send(block, block, q_out.at[0], q_in.at[0], neighbour).wait_recv()
+        for j, later in enumerate(order):
+            if j and i == max(0, 2 * j - 4):
+                q_send(later).start()
         for taken in take.get(i, []):
             arrive(taken)
         if not mine and k < lines:
@@ -369,8 +371,10 @@
 
     def after(i):
         mine, k = turns[i]
-        if not mine:
+        if not mine and k < lines:
             pair_send(k, i).start()
+        if i == min(1, len(turns) - 2):
+            pair_send(lines, 0).start()
         for done in combine.get(i, []):
             pair_send(done, i).wait_recv()
             joined[done] = pack(
@@ -446,7 +450,7 @@
             pltpu.VMEM((lines + 1,) + tile, bf16),
             pltpu.VMEM((lines,) + tile, bf16),
             pltpu.VMEM((lines,) + tile, bf16),
-            dma((keys // math.gcd(keys, 512),)),
+            dma((keys // math.gcd(keys, STEP),)),
             dma((lines,)), dma((lines,)),
             dma((lines,)), dma((lines,)),
             dma((lines + 1,)), dma((lines + 1,)),

time: 171 us -> 163 us (0.953)
  Pallas kernels: 169 us -> 161 us
    pallas_call x1, Pallas kernels: 67.7 us -> 62.2 us  [late_stage(): pl.pallas_call(functools.partial(late_kernel, toks=toks, heads=heads, hea...]
    pallas_call x1, Pallas kernels: 101 us -> 98.8 us  [cross(): pl.pallas_call(functools.partial(cross_kernel, toks=toks, heads=heads, he...]
where the time goes in v4:
time: 163 us
  Pallas kernels  161 us (99%)
  local copies, waits for them, and re-layouts  1.67 us (1%)
    pallas_call x1, Pallas kernels, cross(): pl.pallas_call(functools.partial(cross_kernel, toks=toks, heads=heads, he...  98.8 us
    pallas_call x1, Pallas kernels, late_stage(): pl.pallas_call(functools.partial(late_kernel, toks=toks, heads=heads, hea...  62.2 us

profile of v4, /device:TPU:0, one launch (start us, length us, event | category | flops | bytes accessed | tf_op | source)
XLA Modules:
  0.0 162.7 jit_solution(15814786633752292271)
XLA Ops:
  0.0 98.8 %cross.1 = (bf16[4,256,128]{2,1,0:T(8,128)(2,1)}, bf16[4,2,128,1024]{3,2,1,0:T(8,128)(2,1)}, bf16[4,6,512,256]{3,2,1,0:T(8,128)(2,1)}, bf16[4,2,128,1024]{3,2,1,0:T(8,128)(2,1)}) custom-call(bf16[128,1024]{1,0:T(8,128)(2,1)} %tri_ref.3, bf16[4096,1024]{1,0:T(8,128)(2,1)} %image_ref.1, bf16[1024,256]{1,0:T(8,128)(2,1)} %wq_ref.1, ...), custom_call_target="tpu_custom_call" | custom-call | tf_op jit(solution)/shard_map/cross/pallas_call | solution.py:435
  98.8 62.2 %late_stage.1 = bf16[128,1024]{1,0:T(8,128)(2,1)} custom-call(bf16[128,1024]{1,0:T(8,128)(2,1)} %tri_ref.3, bf16[4,256,128]{2,1,0:T(8,128)(2,1)} %get-tuple-element.9.mixed_ref, bf16[4,2,128,1024]{3,2,1,0:T(8,128)(2,1)} %get-tuple-element.10.cross_out_ref, bf16[4,3,1024,256]{3,2,1,0:T(8,128)(2,1)} %bitcast.4, ...), custom_call_target="tpu_custom_call" | custom-call | tf_op jit(solution)/shard_map/late_stage/pallas_call | solution.py:928
  161.1 1.7 %copy.11 = bf16[128,1024]{1,0:T(8,128)(2,1)} copy(bf16[128,1024]{1,0:T(8,128)(2,1)} %late_stage.1) | data formatting | bytes 524288

commit v5 on v4

--- a/solution.py
+++ b/solution.py
@@ -898,7 +898,12 @@
     for k in range(1, place.pairs):
         gather.near_arrival(k).wait_recv()
     for k in range(1, place.pairs):
-        mlp(k)
+        for side in (1 - place.core, place.core):
+            x = gather.rows[place.pair_at(k) * 2 + side]
+            hidden = jax.nn.gelu(dot(x, win[...]), approximate=True).astype(bf16)
+            scatter.part[k, side] = dot(hidden, down[...]).astype(bf16)
+            if side is not place.core:
+                scatter.near(k).start()
     for k in range(1, place.pairs):
         scatter.relay(k)
     out_ref[...] = (stream + scatter.finish()).astype(bf16)

time: 163 us -> 162 us (level)
  no operation moved by 1% of the time
where the time goes in v5:
time: 162 us
  Pallas kernels  161 us (99%)
  local copies, waits for them, and re-layouts  1.67 us (1%)
    pallas_call x1, Pallas kernels, cross(): pl.pallas_call(functools.partial(cross_kernel, toks=toks, heads=heads, he...  98.8 us
    pallas_call x1, Pallas kernels, late_stage(): pl.pallas_call(functools.partial(late_kernel, toks=toks, heads=heads, hea...  61.8 us

profile of v5, /device:TPU:0, one launch (start us, length us, event | category | flops | bytes accessed | tf_op | source)
XLA Modules:
  0.0 162.3 jit_solution(9500545232660712021)
XLA Ops:
  0.0 98.8 %cross.1 = (bf16[4,256,128]{2,1,0:T(8,128)(2,1)}, bf16[4,2,128,1024]{3,2,1,0:T(8,128)(2,1)}, bf16[4,6,512,256]{3,2,1,0:T(8,128)(2,1)}, bf16[4,2,128,1024]{3,2,1,0:T(8,128)(2,1)}) custom-call(bf16[128,1024]{1,0:T(8,128)(2,1)} %tri_ref.3, bf16[4096,1024]{1,0:T(8,128)(2,1)} %image_ref.1, bf16[1024,256]{1,0:T(8,128)(2,1)} %wq_ref.1, ...), custom_call_target="tpu_custom_call" | custom-call | tf_op jit(solution)/shard_map/cross/pallas_call | solution.py:435
  98.8 61.8 %late_stage.1 = bf16[128,1024]{1,0:T(8,128)(2,1)} custom-call(bf16[128,1024]{1,0:T(8,128)(2,1)} %tri_ref.3, bf16[4,256,128]{2,1,0:T(8,128)(2,1)} %get-tuple-element.9.mixed_ref, bf16[4,2,128,1024]{3,2,1,0:T(8,128)(2,1)} %get-tuple-element.10.cross_out_ref, bf16[4,3,1024,256]{3,2,1,0:T(8,128)(2,1)} %bitcast.4, ...), custom_call_target="tpu_custom_call" | custom-call | tf_op jit(solution)/shard_map/late_stage/pallas_call | solution.py:933
  160.6 1.7 %copy.11 = bf16[128,1024]{1,0:T(8,128)(2,1)} copy(bf16[128,1024]{1,0:T(8,128)(2,1)} %late_stage.1) | data formatting | bytes 524288
